TPU v7x, 32 devices: a whole 2x2x4 slice. The times are simulated.
32 devices in a mesh: groups: 2 (over x), seq: 8 (over z, y), slab: 2 (over core).
Axes of the slice: x: 2, y: 2, z: 4, core: 2. Of those that a mesh axis runs over, the one named last changes fastest.
Arguments:
- noise: float32 [128, 64], P(('groups', 'seq')), parts along dimension 0, may hold values from -6 to 6
- timesteps: int32 [4, 4], P('groups'), parts along dimension 0, may hold values from 0 to 999, as said below
- fine_counts: int32 [4], P('groups'), parts along dimension 0, may hold values from 1 to 3
- w_in: bfloat16 [64, 2560], replicated, may hold values from -0.75 to 0.75
- w_query: bfloat16 [2560, 1024], P(None, 'seq'), may hold values from -24 to 24
- w_key: bfloat16 [2560, 1024], P(None, 'seq'), may hold values from -0.125 to 0.125
- w_value: bfloat16 [2560, 1024], P(None, 'seq'), may hold values from -0.125 to 0.125
- w_out: bfloat16 [1024, 2560], P('seq'), may hold values from -0.1875 to 0.1875
- w_final: float32 [2560, 64], replicated, may hold values from -0.125 to 0.125
- mod_scale: float32 [2560], replicated, may hold values from -0.9 to 0.9
- mod_shift: float32 [2560], replicated, may hold values from -3 to 3
- skip_gain: float32 [2560], replicated, may hold values from 0.3 to 1.2
Outputs:
- slab_ends: float32 [2, 128, 64], P('slab', ('groups', 'seq')), parts along dimension 1
There are 2 independent parts, one for each index of `groups`. A program takes and returns all parts, laid end to end along the dimension named above; an argument that names none is the same for every part. Nothing has to cross between parts.
Inputs may be any that keep to these rules, and one draw needn't show every extreme that they name: `timesteps`: within a slab the points up to column fine_counts strictly fall; the last used point of a slab is the first point of the next; some slab takes exactly 3 steps.
All inputs are finite; a program needn't handle non-finite values.
Results may differ from a plain program's by a relative error of at most 0.013.
Values may be sent and summed in bfloat16 or wider, within the bound.
No kernel may reach another device: no remote copies, remote signals or barrier semaphores. Data moves between devices by JAX's collectives and lax.ppermute only.
A program may use at most 64 MiB of HBM per device.

v0:
```python
import math

import jax
import jax.numpy as jnp
from jax import lax
from jax.sharding import PartitionSpec as P

HEAD_SIZE = 128


def passed_along(value, axis, steps):
    count = lax.axis_size(axis)
    initial, last = (max(0, -steps), min(count, count - steps))
    return lax.ppermute(value, axis, [(source, source + steps) for source in range(initial, last)])


def attend(queries, key_rows, value_rows, head_size):
    row_total, col_count = queries.shape
    head_count = col_count // head_size
    block_rows = min(512, row_total)
    score_scale = 1.0 / math.sqrt(head_size)

    def split_heads(matrix):
        return matrix.reshape(row_total, head_count, head_size).transpose(1, 0, 2)

    def one_head(triple):
        head_query, head_key, head_value = triple
        blocked = head_query.reshape(row_total // block_rows, block_rows, head_size)

        def one_block(query_block):
            scores = (
                jnp.dot(query_block, head_key.T, preferred_element_type=jnp.float32) * score_scale
            )
            row_top = jnp.max(scores, axis=-1, keepdims=True)
            raised = jnp.exp(scores - row_top)
            weights = (raised / jnp.sum(raised, axis=-1, keepdims=True)).astype(jnp.bfloat16)
            return jnp.dot(weights, head_value, preferred_element_type=jnp.float32).astype(
                jnp.bfloat16
            )

        return lax.map(one_block, blocked).reshape(row_total, head_size)

    merged = lax.map(
        one_head, (split_heads(queries), split_heads(key_rows), split_heads(value_rows))
    )
    return merged.transpose(1, 0, 2).reshape(row_total, col_count)


def lift(rounded, noise_level, w_in, mod_scale, mod_shift):
    hidden = jnp.dot(rounded, w_in, preferred_element_type=jnp.float32)
    squares = jnp.mean(hidden * hidden, axis=-1, keepdims=True)
    normed = hidden * lax.rsqrt(squares + 1e-06)
    modulated = (normed * (1.0 + noise_level * mod_scale) + noise_level * mod_shift).astype(
        jnp.bfloat16
    )
    return (normed, modulated)


def project_three(modulated, w_query, w_key, w_value):
    return jnp.stack(
        [
            jnp.dot(modulated, w_query, preferred_element_type=jnp.float32).astype(jnp.bfloat16),
            jnp.dot(modulated, w_key, preferred_element_type=jnp.float32).astype(jnp.bfloat16),
            jnp.dot(modulated, w_value, preferred_element_type=jnp.float32).astype(jnp.bfloat16),
        ]
    )


def velocity(latent, noise_level, params):
    w_in, w_query, w_key, w_value, w_out, w_final, mod_scale, mod_shift, skip_gain = params
    rounded = latent.astype(jnp.bfloat16)
    normed, modulated = lift(rounded, noise_level, w_in, mod_scale, mod_shift)
    stacked = project_three(
        lax.all_gather(modulated, "seq", axis=0, tiled=True), w_query, w_key, w_value
    )
    attended = attend(stacked[0], stacked[1], stacked[2], HEAD_SIZE)
    folded = jnp.dot(
        w_out.astype(jnp.float32),
        w_final,
        precision=lax.Precision.HIGHEST,
        preferred_element_type=jnp.float32,
    )
    rows_here = attended.astype(jnp.float32)
    summed = lax.psum_scatter(
        jnp.dot(
            rows_here, folded, precision=lax.Precision.HIGHEST, preferred_element_type=jnp.float32
        ),
        "seq",
        scatter_dimension=0,
        tiled=True,
    )
    return summed + jnp.dot(
        skip_gain * normed,
        w_final,
        precision=lax.Precision.HIGHEST,
        preferred_element_type=jnp.float32,
    )


def local(
    noise,
    timesteps,
    fine_counts,
    w_in,
    w_query,
    w_key,
    w_value,
    w_out,
    w_final,
    mod_scale,
    mod_shift,
    skip_gain,
):
    params = (w_in, w_query, w_key, w_value, w_out, w_final, mod_scale, mod_shift, skip_gain)
    slab_index = lax.axis_index("slab")
    sigmas = (
        lax.dynamic_index_in_dim(timesteps, slab_index, 0, keepdims=False).astype(jnp.float32)
        / 1000.0
    )
    own_count = lax.dynamic_index_in_dim(fine_counts, slab_index, 0, keepdims=False)
    fine_most = sigmas.shape[0] - 1
    columns = jnp.arange(fine_most + 1)
    final_level = jnp.sum(jnp.where(columns == own_count, sigmas, 0.0))

    def coarse(latent):
        return latent + (final_level - sigmas[0]) * velocity(latent, sigmas[0], params)

    def advance(ended):
        arrived = passed_along(ended, "slab", 1)
        return jnp.where(slab_index == 0, noise, arrived)

    starts = noise
    starts = advance(coarse(starts))
    ended = noise
    coarse_now = coarse(starts)
    latent = starts
    for fine_step in range(fine_most):
        step_size = jnp.where(fine_step < own_count, sigmas[fine_step + 1] - sigmas[fine_step], 0.0)
        latent = latent + step_size * velocity(latent, sigmas[fine_step], params)
    correction = latent - coarse_now
    ended = coarse_now + correction
    starts = advance(ended)
    ended = coarse(starts) + correction
    return ended[None]


def solution(mesh):
    placed = (
        P(("groups", "seq"), None),
        P("groups", None),
        P("groups"),
        P(),
        P(None, "seq"),
        P(None, "seq"),
        P(None, "seq"),
        P("seq", None),
        P(),
        P(),
        P(),
        P(),
    )
    return jax.shard_map(
        local,
        mesh=mesh,
        in_specs=placed,
        out_specs=P("slab", ("groups", "seq"), None),
        check_vma=False,
    )
```

profile of v0, /device:TPU:0, one launch (start us, length us, event | category | flops | bytes accessed | tf_op | source)
XLA Modules:
  0.0 360.6 jit_solution(8428589700861357536)
XLA Ops:
  0.0 0.0 copy-start
  0.0 1.3 dynamic_slice.58
  1.3 2.0 fusion.57
  3.3 0.7 fusion.58
  4.0 1.3 multiply_reduce_fusion.4
  6.5 2.6 multiply_add_fusion
  9.1 0.1 add_convert_fusion.4
  9.1 32.7 %all_gather.16 = bf16[64,2560]{1,0:T(8,128)(2,1)S(1)} all-gather(bf16[8,2560]{1,0:T(8,128)(2,1)S(1)} %add_convert_fusion.4), channel_id=1, replica_groups=mesh['groups'=2,'seq'=8,'slab'=2] {'seq'}, dimensions={0}, use_global_device_ids=true | all-gather | bytes 368640 | tf_op jit(solution)/shard_map/all_gather | solution.py:74
  41.8 0.0 copy-done.1
  41.8 1.9 fusion.64
  43.7 0.0 copy-done
  43.7 0.0 copy-start.2
  43.7 0.2 convolution_convert_fusion.18
  44.0 0.8 copy-done.2
  44.8 0.4 fusion.59
  45.2 0.7 copy-done.3
  45.9 0.4 convolution_convert_fusion.16
  46.2 0.2 fusion.65
  46.4 37.2 %all-reduce = f32[64,64]{1,0:T(8,128)S(1)} all-reduce(f32[64,64]{1,0:T(8,128)S(1)} %fusion.65), channel_id=2, replica_groups=mesh['groups'=2,'seq'=8,'slab'=2] {'seq'}, use_global_device_ids=true, to_apply=%region_4.5.clone | all-reduce | flops 4096 | bytes 32768
  83.6 0.7 copy-done.7
  84.3 0.6 dynamic-slice.20
  85.5 0.0 copy-done.5
  85.5 0.0 copy-start.4
  85.5 0.7 fusion.10
  86.2 1.3 collective-permute-start
  93.2 0.0 collective-permute-done
  93.2 0.3 multiply_reduce_fusion.3
  93.5 0.1 add_convert_fusion.3
  93.6 30.9 %all_gather.17 = bf16[64,2560]{1,0:T(8,128)(2,1)S(1)} all-gather(bf16[8,2560]{1,0:T(8,128)(2,1)S(1)} %add_convert_fusion.3), channel_id=1, replica_groups=mesh['groups'=2,'seq'=8,'slab'=2] {'seq'}, dimensions={0}, use_global_device_ids=true | all-gather | bytes 368640 | tf_op jit(solution)/shard_map/all_gather | solution.py:74
  124.5 0.2 convolution_convert_fusion.14
  124.7 0.4 fusion.60
  125.2 0.4 convolution_convert_fusion.12
  125.5 0.2 fusion.66
  125.7 33.1 %all-reduce.1 = f32[64,64]{1,0:T(8,128)S(1)} all-reduce(f32[64,64]{1,0:T(8,128)S(1)} %fusion.66), channel_id=3, replica_groups=mesh['groups'=2,'seq'=8,'slab'=2] {'seq'}, use_global_device_ids=true, to_apply=%region_8.9.clone | all-reduce | flops 4096 | bytes 32768
  158.8 0.7 convolution_add_fusion.3
  159.5 0.3 multiply_reduce_fusion.2
  159.8 0.1 add_convert_fusion.2
  159.9 30.9 %all_gather.18 = bf16[64,2560]{1,0:T(8,128)(2,1)S(1)} all-gather(bf16[8,2560]{1,0:T(8,128)(2,1)S(1)} %add_convert_fusion.2), channel_id=1, replica_groups=mesh['groups'=2,'seq'=8,'slab'=2] {'seq'}, dimensions={0}, use_global_device_ids=true | all-gather | bytes 368640 | tf_op jit(solution)/shard_map/all_gather | solution.py:74
  190.7 0.2 convolution_convert_fusion.10
  191.0 0.4 fusion.61
  191.4 0.4 convolution_convert_fusion.8
  191.8 0.2 fusion.67
  191.9 33.0 %all-reduce.2 = f32[64,64]{1,0:T(8,128)S(1)} all-reduce(f32[64,64]{1,0:T(8,128)S(1)} %fusion.67), channel_id=4, replica_groups=mesh['groups'=2,'seq'=8,'slab'=2] {'seq'}, use_global_device_ids=true, to_apply=%region_12.13.clone | all-reduce | flops 4096 | bytes 32768
  225.0 0.7 fusion.8
  225.7 0.3 multiply_reduce_fusion.1
  225.9 0.1 add_convert_fusion.1
  226.0 30.9 %all_gather.19 = bf16[64,2560]{1,0:T(8,128)(2,1)S(1)} all-gather(bf16[8,2560]{1,0:T(8,128)(2,1)S(1)} %add_convert_fusion.1), channel_id=1, replica_groups=mesh['groups'=2,'seq'=8,'slab'=2] {'seq'}, dimensions={0}, use_global_device_ids=true | all-gather | bytes 368640 | tf_op jit(solution)/shard_map/all_gather | solution.py:74
  256.9 0.2 convolution_convert_fusion.6
  257.1 0.4 fusion.62
  257.5 0.4 convolution_convert_fusion.4
  257.9 0.2 fusion.68
  258.1 33.0 %all-reduce.3 = f32[64,64]{1,0:T(8,128)S(1)} all-reduce(f32[64,64]{1,0:T(8,128)S(1)} %fusion.68), channel_id=5, replica_groups=mesh['groups'=2,'seq'=8,'slab'=2] {'seq'}, use_global_device_ids=true, to_apply=%region_16.17.clone | all-reduce | flops 4096 | bytes 32768
  291.1 0.7 fusion.56
  291.8 1.3 collective-permute-start.1
  293.1 0.8 collective-permute-done.1
  293.9 0.3 multiply_reduce_fusion
  294.2 0.1 add_convert_fusion
  294.3 30.9 %all_gather.20 = bf16[64,2560]{1,0:T(8,128)(2,1)S(1)} all-gather(bf16[8,2560]{1,0:T(8,128)(2,1)S(1)} %add_convert_fusion), channel_id=1, replica_groups=mesh['groups'=2,'seq'=8,'slab'=2] {'seq'}, dimensions={0}, use_global_device_ids=true | all-gather | bytes 368640 | tf_op jit(solution)/shard_map/all_gather | solution.py:74
  325.1 0.2 convolution_convert_fusion.2
  325.4 0.4 fusion.63
  325.8 0.4 convolution_convert_fusion
  326.2 0.2 fusion.69
  326.3 33.0 %all-reduce.4 = f32[64,64]{1,0:T(8,128)S(1)} all-reduce(f32[64,64]{1,0:T(8,128)S(1)} %fusion.69), channel_id=6, replica_groups=mesh['groups'=2,'seq'=8,'slab'=2] {'seq'}, use_global_device_ids=true, to_apply=%region_20.21.clone | all-reduce | flops 4096 | bytes 32768
  359.4 1.3 fusion.3
  (18 shorter events, 0.3 us)
Async XLA Ops:
  0.0 43.7 %copy-start = (bf16[2560,128]{1,0:T(8,128)(2,1)S(1)}, bf16[2560,128]{1,0:T(8,128)(2,1)}, u32[]{:S(2)}) copy-start(bf16[2560,128]{1,0:T(8,128)(2,1)} %param.17) | copy-start | bytes 1966084
  0.0 41.8 %copy-start.1 = (f32[2560,64]{0,1:T(8,128)S(1)}, f32[2560,64]{0,1:T(8,128)}, u32[]{:S(2)}) copy-start(f32[2560,64]{0,1:T(8,128)} %param.20) | copy-start | bytes 1966084
  43.7 1.1 copy-start.2
  44.8 1.1 copy-start.3
  83.6 1.9 copy-start.5
  83.6 0.7 copy-start.7
  84.3 1.2 copy-start.6
  85.5 7.7 %copy-start.4 = (bf16[64,2560]{1,0:T(8,128)(2,1)S(1)}, bf16[64,2560]{1,0:T(8,128)(2,1)}, u32[]{:S(2)}) copy-start(bf16[64,2560]{1,0:T(8,128)(2,1)} %param.15) | copy-start | bytes 983044
  86.2 7.0 %collective-permute-start = (f32[8,64]{1,0:T(8,128)S(1)}, f32[8,64]{1,0:T(8,128)S(1)}, u32[]{:S(2)}, u32[]{:S(2)}) collective-permute-start(f32[8,64]{1,0:T(8,128)S(1)} %fusion.10), channel_id=1, source_target_pairs={{0,1},{2,3},{4,5},{6,7},{8,9},{10,11},{12,13},{14,15},{16,17},{18,... | collective-permute-start | bytes 6152 | tf_op jit(solution)/shard_map/ppermute | solution.py:14
  291.8 2.1 collective-permute-start.1
where the time goes:
time: 361 us
  blocking collectives  325 us (90%)
  matrix products  14 us (4%)
  between operations  7.77 us (2%)
  other arithmetic  5.2 us (1%)
  local copies, waits for them, and re-layouts  4.82 us (1%)
    unnamed x5, blocking collectives  169 us
    all_gather x5, blocking collectives, velocity(): lax.all_gather(modulated, 'seq', axis=0, tiled=True)  156 us
  transfers between devices with their start and end apart: 2, of which 1 were waited for; matrix products, arithmetic and copies ran while one was open for 0% of the time, Pallas kernels for 0%

commit v1 on v0

v1 whole, which is shorter than its diff:
```python
import functools
import math

import jax
import jax.numpy as jnp
from jax import lax
from jax.experimental import pallas as pl
from jax.experimental.pallas import tpu as pltpu
from jax.sharding import PartitionSpec as P

HEAD_SIZE = 128
F32 = jnp.float32
BF16 = jnp.bfloat16
NT = (((1,), (1,)), ((), ()))
TN = (((0,), (0,)), ((), ()))


def dot(a, b, dims=None, precision=None):
    if dims is None:
        dims = (((1,), (0,)), ((), ()))
    return lax.dot_general(a, b, dims, precision=precision, preferred_element_type=F32)


def split2(x):
    high = x.astype(BF16)
    return high, (x - high.astype(F32)).astype(BF16)


def split3(x):
    high, _ = split2(x)
    rest = x - high.astype(F32)
    mid, low = split2(rest)
    return high, mid, low


def dot_fine(a, b):
    a_high, a_low = split2(a)
    b_high, b_low = split2(b)
    return dot(
        jnp.concatenate([a_high, a_high, a_low], axis=1),
        jnp.concatenate([b_high, b_low, b_high], axis=1),
        NT,
    )


def payload_rows(channels):
    return channels + channels // 2 + 16


def fold_kernel(
    noise_ref,
    w_in_hbm,
    wq_hbm,
    wk_hbm,
    wv_hbm,
    wo_hbm,
    wf_hbm,
    scale_ref,
    shift_ref,
    out_ref,
    w_in,
    lift,
    w_a,
    w_b,
    wo,
    wf,
    wf2,
    sems,
    *,
    chunks,
):
    slab = lax.axis_index("slab")
    channels, width = w_in.shape
    depth = width // chunks
    half = channels // 2

    def fetch(src, dst, index):
        copy = pltpu.make_async_copy(src, dst, sems.at[index])
        copy.start()
        return copy

    def build_lift():
        base = w_in[...].astype(F32)
        high, low = split2(base * scale_ref[...])
        lift[0:channels] = w_in[...]
        lift[channels : 2 * channels] = high
        lift[2 * channels : 3 * channels] = low
        shift_high, shift_low = split2(shift_ref[...])
        row = lax.broadcasted_iota(jnp.int32, (16, width), 0)
        tail = jnp.where(
            row == 0,
            shift_high.astype(F32),
            jnp.where(row == 1, shift_low.astype(F32), 0.0),
        )
        lift[3 * channels : 3 * channels + 16] = tail.astype(BF16)

    def parts(total):
        first = total[0:channels]
        second = total[channels : 2 * channels] + total[2 * channels : 3 * channels]
        tail = total[3 * channels : 3 * channels + 8]
        third = tail[0:1] + tail[1:2]
        return first, second, third

    def zero_rows(count):
        return jnp.zeros((count, 2 * channels), F32)

    @pl.when(slab == 0)
    def _():
        first = fetch(w_in_hbm, w_in, 0)
        copies = []
        for c in range(chunks):
            rows = pl.ds(c * depth, depth)
            copies.append(
                (
                    fetch(wq_hbm.at[rows], w_a.at[rows], 1 + 2 * c),
                    fetch(wk_hbm.at[rows], w_b.at[rows], 2 + 2 * c),
                )
            )
        first.wait()
        build_lift()
        total = None
        for c in range(chunks):
            rows = slice(c * depth, (c + 1) * depth)
            for copy in copies[c]:
                copy.wait()
            term = dot(lift[:, rows], jnp.concatenate([w_a[rows], w_b[rows]], axis=1))
            total = term if total is None else total + term
        q0, q1, q2 = parts(total[:, 0:HEAD_SIZE] * (1.0 / math.sqrt(HEAD_SIZE)))
        k0, k1, k2 = parts(total[:, HEAD_SIZE : 2 * HEAD_SIZE])
        pad = jnp.zeros((7, HEAD_SIZE), F32)
        q_all = jnp.concatenate([q0, q1], axis=0)
        k_all = jnp.concatenate([k0, k1], axis=0)
        form = dot_fine(k_all, q_all)
        k_last = jnp.concatenate([k2, pad], axis=0)
        q_last = jnp.concatenate([q2, pad], axis=0)
        a_rows = dot_fine(k_last, q_all)[0:1]
        b_rows = dot_fine(q_last, k_all)[0:1]
        constant = jnp.sum(k2 * q2)
        lane = lax.broadcasted_iota(jnp.int32, (channels, 2 * channels), 1)
        top, bottom = form[0:channels], form[channels : 2 * channels]
        rolled = pltpu.roll(bottom, channels, 1)
        out_ref[0:channels] = jnp.where(lane < channels, top, top + rolled).astype(BF16)
        out_ref[channels : channels + half] = jnp.where(
            lane[0:half] < channels, rolled[0:half], bottom[half:channels]
        ).astype(BF16)
        lane = lax.broadcasted_iota(jnp.int32, (16, 2 * channels), 1)
        row = lax.broadcasted_iota(jnp.int32, (16, 2 * channels), 0)
        a_roll = pltpu.roll(jnp.broadcast_to(a_rows, (8, 2 * channels)), channels, 1)[0:1]
        b_roll = pltpu.roll(jnp.broadcast_to(b_rows, (8, 2 * channels)), channels, 1)[0:1]
        left = lane < channels
        tile_one = jnp.where(left, 0.0, a_roll)
        tile_two = jnp.where(left, a_roll, 0.0)
        at_const = (lane == channels + 2) | (lane == channels + 3)
        tile_two = jnp.where(at_const, constant, tile_two)
        ext = jnp.where(
            row == 0,
            tile_one,
            jnp.where(
                row == 1,
                tile_two,
                jnp.where(row == 2, b_rows, jnp.where(row == 3, b_roll, 0.0)),
            ),
        )
        out_ref[channels + half : channels + half + 16] = ext.astype(BF16)

    @pl.when(slab != 0)
    def _():
        first = fetch(w_in_hbm, w_in, 0)
        second = fetch(wf_hbm, wf, 1)
        third = fetch(wo_hbm, wo, 2)
        copies = []
        for c in range(chunks):
            rows = pl.ds(c * depth, depth)
            copies.append(fetch(wv_hbm.at[rows], w_a.at[rows], 3 + c))
        first.wait()
        build_lift()
        second.wait()
        high, low = split2(wf[...])
        wf2[0:channels] = high
        wf2[channels : 2 * channels] = low
        third.wait()
        both = dot(wf2[...], wo[...], NT)
        out_t = both[0:channels] + both[channels : 2 * channels]
        total = None
        for c in range(chunks):
            rows = slice(c * depth, (c + 1) * depth)
            copies[c].wait()
            term = dot(lift[:, rows], w_a[rows])
            total = term if total is None else total + term
        v0, v1, v2 = parts(total)
        out_ref[0:channels] = dot_fine(out_t, jnp.concatenate([v0, v1], axis=0)).astype(BF16)
        v_last = jnp.concatenate([v2, jnp.zeros((7, HEAD_SIZE), F32)], axis=0)
        p_row = dot_fine(v_last, jnp.concatenate([out_t, out_t], axis=0))[0:1]
        row = lax.broadcasted_iota(jnp.int32, (16, 2 * channels), 0)
        out_ref[channels : channels + 16] = jnp.where(row == 0, p_row, 0.0).astype(BF16)
        tokens = noise_ref.shape[0]
        n_high, n_mid, n_low = split3(noise_ref[...])
        pieces = jnp.concatenate(
            [
                jnp.concatenate([n_high.astype(F32), n_mid.astype(F32)], axis=1),
                jnp.concatenate([n_low.astype(F32), jnp.zeros_like(noise_ref[...])], axis=1),
            ],
            axis=0,
        )
        out_ref[channels + 16 : channels + 16 + 2 * tokens] = pieces.astype(BF16)


def side_kernel(w_in_ref, wf_ref, gain_ref, out_ref):
    channels, width = w_in_ref.shape
    w_in = w_in_ref[...]
    gram = dot(w_in, w_in, NT) * (1.0 / width)
    g_high, g_mid, g_low = split3(gram)
    gained = w_in.astype(F32) * gain_ref[...]
    s_high, s_low = split2(dot_fine(wf_ref[...], gained))
    out_ref[...] = jnp.concatenate([g_high, g_mid, g_low, s_high, s_low], axis=0)


def solve_kernel(
    times_ref,
    counts_ref,
    noise_ref,
    own_ref,
    other_ref,
    side_ref,
    out_ref,
    t1,
    t2,
    t3,
    a1,
    a2,
    start,
    *,
    heads,
):
    slab = lax.axis_index("slab")
    tokens, channels = noise_ref.shape
    count = start.shape[1]
    lanes = 2 * count
    half = channels // 2
    rows = payload_rows(channels)
    fine_most = times_ref.shape[1] - 1
    first_slab = slab == 0

    wide = lax.broadcasted_iota(jnp.int32, (channels, 2 * channels), 1)
    sel_row = lax.broadcasted_iota(jnp.int32, (16, 2 * channels), 0)
    sel_lane = lax.broadcasted_iota(jnp.int32, (16, 2 * channels), 1) - channels

    def pick(cond):
        return jnp.where(cond, 1.0, 0.0).astype(BF16)

    b_pick = pick(
        ((sel_row == 2) & ((sel_lane == 0) | (sel_lane == 1)))
        | ((sel_row == 3) & ((sel_lane == 2) | (sel_lane == 3)))
    )
    p_pick = pick((sel_row == 0) & ((sel_lane == 4) | (sel_lane == 5)))
    for h in range(heads):
        base = h * rows

        def score_side(lo, n):
            at = pl.ds(base + lo, n)
            return jnp.where(first_slab, own_ref[at].astype(F32), other_ref[at].astype(F32))

        def value_side(lo, n):
            at = pl.ds(base + lo, n)
            return jnp.where(first_slab, other_ref[at].astype(F32), own_ref[at].astype(F32))

        to = pl.ds(h * channels, channels)
        t1[to] = score_side(0, channels).astype(BF16)
        folded = score_side(channels, half)
        square = jnp.concatenate([folded, pltpu.roll(folded, channels, 1)], axis=0)
        ext = score_side(channels + half, 16)
        p_ext = value_side(channels, 16)
        columns = dot(ext[:, 0:channels].astype(BF16), b_pick, TN) + dot(
            p_ext[:, 0:channels].astype(BF16), p_pick, TN
        )
        t2[to] = jnp.where(wide < channels, square, columns).astype(BF16)
        a1[h : h + 1] = ext[0:1]
        a2[h : h + 1] = ext[1:2]
        t3[to] = value_side(0, channels).astype(BF16)
        pieces = value_side(channels + 16, 2 * tokens)
        upper, lower = pieces[0:tokens], pieces[tokens : 2 * tokens]
        whole = (upper + pltpu.roll(upper, channels, 1)) + lower
        start[:, pl.ds(h * tokens, tokens)] = jnp.transpose(whole)[0:channels]

    lane = lax.broadcasted_iota(jnp.int32, (1, lanes), 1)
    left = lane < count

    def level(slab_id, column):
        return (jnp.zeros((1, lanes), jnp.int32) + times_ref[slab_id, column]).astype(F32) / 1000.0

    def step(slab_id, j):
        size = level(slab_id, j + 1) - level(slab_id, j)
        return jnp.where(j < counts_ref[slab_id], size, 0.0)

    def span(slab_id):
        last = jnp.zeros((1, lanes), F32)
        for column in range(fine_most + 1):
            last = jnp.where(column == counts_ref[slab_id], level(slab_id, column), last)
        return last - level(slab_id, 0)

    def velocity(u, s):
        rounded = u.astype(BF16)
        sides = dot(side_ref[...], rounded)
        form = (
            sides[0:channels] + sides[channels : 2 * channels]
        ) + sides[2 * channels : 3 * channels]
        squares = jnp.sum(form * rounded.astype(F32), axis=0, keepdims=True)
        r = lax.rsqrt(jnp.maximum(squares, 0.0) + 1e-06)
        skip = r * (sides[3 * channels : 4 * channels] + sides[4 * channels : 5 * channels])
        x = r * rounded.astype(F32)
        s2 = s * s
        s_high, s_low = split2(s)
        s2_high, s2_low = split2(s2)
        row = lax.broadcasted_iota(jnp.int32, (channels, lanes), 0)
        s_rows = jnp.where(
            row == 0,
            s_high.astype(F32),
            jnp.where(
                row == 1,
                s_low.astype(F32),
                jnp.where(
                    row == 2, s2_high.astype(F32), jnp.where(row == 3, s2_low.astype(F32), 0.0)
                ),
            ),
        )
        p_rows = jnp.where(
            row == 4, s_high.astype(F32), jnp.where(row == 5, s_low.astype(F32), 0.0)
        )
        x_one = jnp.concatenate([x, s * x], axis=0).astype(BF16)
        x_two = jnp.concatenate([s2 * x, s_rows], axis=0).astype(BF16)
        x_p = jnp.concatenate([jnp.zeros_like(x), p_rows], axis=0).astype(BF16)
        query = (dot(t1[...], x_one) + dot(t2[...], x_two)).astype(BF16)
        value = (dot(t3[...], x_one) + dot(t2[...], x_p)).astype(BF16)
        column_terms = dot(a1[...].astype(BF16), x_one) + dot(a2[...].astype(BF16), x_two)
        keys = jnp.transpose(x).astype(BF16)
        lhs, rhs = [], []
        for h in range(heads):
            at = slice(h * channels, (h + 1) * channels)
            both = dot(keys, query[at])
            scores = jnp.where(left, both[0:count], both[count:lanes]) + column_terms[h : h + 1]
            raised = jnp.exp(scores - jnp.max(scores, axis=0, keepdims=True))
            weights = raised / jnp.sum(raised, axis=0, keepdims=True)
            lhs.append(value[at])
            rhs.append(jnp.where(left, weights, 0.0).astype(BF16))
            rhs.append(jnp.where(left, 0.0, weights).astype(BF16))
        return skip + dot(jnp.concatenate(lhs, axis=1), jnp.concatenate(rhs, axis=0))

    noise = jnp.concatenate([start[...], start[...]], axis=1)
    moved = velocity(noise, level(0, 0))
    first_coarse = noise + span(0) * moved
    u = jnp.where(left, noise + step(0, 0) * moved, first_coarse)
    coarse_old = None
    for j in range(fine_most):
        last = j == fine_most - 1
        s = jnp.where(left, level(1, 0) if last else level(0, j + 1), level(1, j))
        moved = velocity(u, s)
        if j == 0:
            coarse_old = u + span(1) * moved
        ahead = span(1) if last else step(0, j + 1)
        if last:
            fine_first = u
        u = u + jnp.where(left, ahead, step(1, j)) * moved
    change = pltpu.roll(u - coarse_old, count, 1)
    end_second = u + change
    end_first = first_coarse + (fine_first - first_coarse)
    ended = jnp.where(first_slab, end_first, end_second)
    out_ref[...] = jnp.transpose(ended)[0:tokens]


def gathered(value, axis):
    size = lax.axis_size(axis)
    stride = size // 2
    while stride:
        pairs = [(i, i ^ stride) for i in range(size)]
        value = jnp.concatenate([value, lax.ppermute(value, axis, pairs)], axis=0)
        stride //= 2
    return value


def local(
    noise,
    timesteps,
    fine_counts,
    w_in,
    w_query,
    w_key,
    w_value,
    w_out,
    w_final,
    mod_scale,
    mod_shift,
    skip_gain,
):
    channels, width = w_in.shape
    tokens = noise.shape[0]
    heads = lax.axis_size("seq")
    count = tokens * heads
    rows = payload_rows(channels)
    wf_t = w_final.T
    row_of = lambda vector: vector.reshape(1, width)
    vmem = pl.BlockSpec(memory_space=pltpu.VMEM)
    smem = pl.BlockSpec(memory_space=pltpu.SMEM)
    hbm = pl.BlockSpec(memory_space=pl.ANY)
    chunks = 5
    packed = pl.pallas_call(
        functools.partial(fold_kernel, chunks=chunks),
        out_shape=jax.ShapeDtypeStruct((rows, 2 * channels), BF16),
        in_specs=[vmem, hbm, hbm, hbm, hbm, hbm, hbm, vmem, vmem],
        out_specs=vmem,
        scratch_shapes=[
            pltpu.VMEM((channels, width), BF16),
            pltpu.VMEM((3 * channels + 16, width), BF16),
            pltpu.VMEM((width, HEAD_SIZE), BF16),
            pltpu.VMEM((width, HEAD_SIZE), BF16),
            pltpu.VMEM((HEAD_SIZE, width), BF16),
            pltpu.VMEM((channels, width), F32),
            pltpu.VMEM((2 * channels, width), BF16),
            pltpu.SemaphoreType.DMA((2 * chunks + 4,)),
        ],
        name="fold",
    )(noise, w_in, w_query, w_key, w_value, w_out, wf_t, row_of(mod_scale), row_of(mod_shift))
    side = pl.pallas_call(
        side_kernel,
        out_shape=jax.ShapeDtypeStruct((5 * channels, channels), BF16),
        in_specs=[vmem, vmem, vmem],
        out_specs=vmem,
        name="side",
    )(w_in, wf_t, row_of(skip_gain))
    own = gathered(packed, "seq")
    other = lax.ppermute(own, "slab", [(0, 1), (1, 0)])
    ended = pl.pallas_call(
        functools.partial(solve_kernel, heads=heads),
        out_shape=jax.ShapeDtypeStruct((tokens, channels), F32),
        in_specs=[smem, smem, vmem, vmem, vmem, vmem],
        out_specs=vmem,
        scratch_shapes=[
            pltpu.VMEM((heads * channels, 2 * channels), BF16),
            pltpu.VMEM((heads * channels, 2 * channels), BF16),
            pltpu.VMEM((heads * channels, 2 * channels), BF16),
            pltpu.VMEM((heads, 2 * channels), F32),
            pltpu.VMEM((heads, 2 * channels), F32),
            pltpu.VMEM((channels, count), F32),
        ],
        name="solve",
    )(timesteps, fine_counts, noise, own, other, side)
    return ended[None]


def solution(mesh):
    placed = (
        P(("groups", "seq"), None),
        P("groups", None),
        P("groups"),
        P(),
        P(None, "seq"),
        P(None, "seq"),
        P(None, "seq"),
        P("seq", None),
        P(),
        P(),
        P(),
        P(),
    )
    return jax.shard_map(
        local,
        mesh=mesh,
        in_specs=placed,
        out_specs=P("slab", ("groups", "seq"), None),
        check_vma=False,
    )
```

time: 361 us -> 31.7 us (0.09)
  blocking collectives: 325 us -> 0 us
  matrix products: 14 us -> 0 us
  Pallas kernels: 0 us -> 11.9 us
  between operations: 7.77 us -> 0.07 us
  waiting for transfers between devices: 0.81 us -> 7.48 us
  starting transfers between devices: 2.58 us -> 7.88 us
  other arithmetic: 5.2 us -> 0.78 us
    unnamed x5 -> x0, blocking collectives: 169 us -> none
    all_gather x5 -> x0, blocking collectives: 156 us -> none  [velocity(): lax.all_gather(modulated, 'seq', axis=0, tiled=True)]
    dot_general x31 -> x0, matrix products: 14 us -> none  [the longest x5 4 us: velocity(): jnp.dot(skip_gain * normed, w_final, precision=lax.Precision.HIGHEST, pre...]
    pallas_call x0 -> x3, Pallas kernels: none -> 11.9 us  [the longest x1 5.7 us: local(): pl.pallas_call(functools.partial(solve_kernel, heads=heads), out_shape=ja...]
    ppermute x2 -> x4, waiting for transfers between devices: 0.81 us -> 7.48 us  [the longest x3 7.48 us: gathered(): value = jnp.concatenate([value, lax.ppermute(value, axis, pairs)], axis=0)]
    ppermute x2 -> x4, starting transfers between devices: 2.58 us -> 7.88 us  [the longest x3 7.81 us: gathered(): value = jnp.concatenate([value, lax.ppermute(value, axis, pairs)], axis=0)]
  transfers between devices with their start and end apart: 2 -> 4, of which waited for: 1 -> 3; matrix products, arithmetic and copies ran while one was open for 0% -> 2% of each run, Pallas kernels for 0% -> 7%
where the time goes in v1:
time: 31.7 us; the launch traced here: 31.4 us
  Pallas kernels  11.9 us (38%)
  starting transfers between devices  7.88 us (25%)
  waiting for transfers between devices  7.48 us (24%)
  local copies, waits for them, and re-layouts  3.24 us (10%)
  other arithmetic  0.78 us (2%)
    ppermute x3, starting transfers between devices, gathered(): value = jnp.concatenate([value, lax.ppermute(value, axis, pairs)], axis=0)  7.81 us
    ppermute x3, waiting for transfers between devices, gathered(): value = jnp.concatenate([value, lax.ppermute(value, axis, pairs)], axis=0)  7.48 us
    pallas_call x1, Pallas kernels, local(): pl.pallas_call(functools.partial(solve_kernel, heads=heads), out_shape=ja...  5.7 us
    pallas_call x1, Pallas kernels, local(): pl.pallas_call(functools.partial(fold_kernel, chunks=chunks), out_shape=j...  3.93 us
    reshape x3, local copies, waits for them, and re-layouts, local(): row_of = lambda vector: vector.reshape(1, width)  2.53 us
    pallas_call x1, Pallas kernels, local(): pl.pallas_call(side_kernel, out_shape=jax.ShapeDtypeStruct((5 * channels,...  2.31 us
    concatenate x3, other arithmetic, gathered(): value = jnp.concatenate([value, lax.ppermute(value, axis, pairs)], axis=0)  0.78 us
    unnamed x10, local copies, waits for them, and re-layouts  0.71 us
  transfers between devices with their start and end apart: 4, of which 3 were waited for; matrix products, arithmetic and copies ran while one was open for 2% of the time, Pallas kernels for 7%

profile of v1, /device:TPU:0, one launch (start us, length us, event | category | flops | bytes accessed | tf_op | source)
XLA Modules:
  0.0 31.4 jit_solution(16634833810164685940)
XLA Ops:
  0.0 0.0 copy-start.3
  0.0 1.3 %reshape.9.scale_ref = f32[1,2560]{1,0:T(1,128)} reshape(f32[2560]{0:T(1024)} %param.21) | data formatting | bytes 20480 | tf_op jit(solution)/shard_map/reshape | solution.py:400
  1.3 0.0 copy-done.3
  1.3 0.6 %reshape.10.shift_ref = f32[1,2560]{1,0:T(1,128)} reshape(f32[2560]{0:T(1024)S(1)} %copy-done.3) | data formatting | bytes 20480 | tf_op jit(solution)/shard_map/reshape | solution.py:400
  1.9 3.9 %fold.1 = bf16[112,128]{1,0:T(8,128)(2,1)} custom-call(f32[8,64]{1,0:T(8,128)} %noise_ref.3, bf16[64,2560]{1,0:T(8,128)(2,1)} %w_in_ref.1, bf16[2560,128]{1,0:T(8,128)(2,1)} %wq_hbm.1, bf16[2560,128]{1,0:T(8,128)(2,1)} %wk_hbm.1, bf16[2560,128]{1,0:T(8,128)(2,1)} %wv_hbm.1, bf16[128,2560]{1,0:T(8,128)(2,1)} %wo_hbm.1, f32[64,2560]{1,0:T(8,128)} %bitcast.2, ...), custom_call_target="tpu_custom_call" | custom-call | tf_op jit(solution)/shard_map/fold/pallas_call | solution.py:405
  5.9 0.0 copy-start.1
  5.9 4.1 %collective-permute-start = (bf16[112,128]{1,0:T(8,128)(2,1)}, bf16[112,128]{1,0:T(8,128)(2,1)S(1)}, u32[]{:S(2)}, u32[]{:S(2)}) collective-permute-start(bf16[112,128]{1,0:T(8,128)(2,1)} %fold.1), channel_id=1, source_target_pairs={{0,8},{2,10},{4,12},{6,14},{8,0},{10,2},{12,4},{14,6},{1,9},{3,11}... | collective-permute-start | bytes 86024 | tf_op jit(solution)/shard_map/ppermute | solution.py:375
  10.0 2.1 %collective-permute-done = bf16[112,128]{1,0:T(8,128)(2,1)S(1)} collective-permute-done((bf16[112,128]{1,0:T(8,128)(2,1)}, bf16[112,128]{1,0:T(8,128)(2,1)S(1)}, u32[]{:S(2)}, u32[]{:S(2)}) %collective-permute-start) | collective-permute-done | bytes 28704 | tf_op jit(solution)/shard_map/ppermute | solution.py:375
  12.1 0.8 %pad_maximum_fusion.2 = bf16[224,128]{1,0:T(8,128)(2,1)S(1)} fusion(bf16[112,128]{1,0:T(8,128)(2,1)S(1)} %collective-permute-done, bf16[112,128]{1,0:T(8,128)(2,1)} %fold.1), kind=kLoop, calls=%fused_computation.2 | loop fusion | flops 114688 | bytes 114688 | tf_op jit(solution)/shard_map/concatenate | solution.py:375
  12.9 1.8 %collective-permute-start.1 = (bf16[224,128]{1,0:T(8,128)(2,1)S(1)}, bf16[224,128]{1,0:T(8,128)(2,1)S(1)}, u32[]{:S(2)}, u32[]{:S(2)}) collective-permute-start(bf16[224,128]{1,0:T(8,128)(2,1)S(1)} %pad_maximum_fusion.2), channel_id=1, source_target_pairs={{0,4},{2,6},{4,0},{6,2},{8,12},{10,14},{12,8},{14,10},{1,5},{3,7},... | collective-permute-start | bytes 172040 | tf_op jit(solution)/shard_map/ppermute | solution.py:375
  14.7 2.3 %collective-permute-done.1 = bf16[224,128]{1,0:T(8,128)(2,1)S(1)} collective-permute-done((bf16[224,128]{1,0:T(8,128)(2,1)S(1)}, bf16[224,128]{1,0:T(8,128)(2,1)S(1)}, u32[]{:S(2)}, u32[]{:S(2)}) %collective-permute-start.1) | collective-permute-done | bytes 57376 | tf_op jit(solution)/shard_map/ppermute | solution.py:375
  17.1 0.0 copy-done.1
  17.1 0.0 copy-start.4
  17.1 1.8 %collective-permute-start.2 = (bf16[448,128]{1,0:T(8,128)(2,1)S(1)}, bf16[448,128]{1,0:T(8,128)(2,1)S(1)}, u32[]{:S(2)}, u32[]{:S(2)}) collective-permute-start(bf16[448,128]{1,0:T(8,128)(2,1)S(1)} %pad_maximum_fusion.1), channel_id=1, source_target_pairs={{0,2},{2,0},{4,6},{6,4},{8,10},{10,8},{12,14},{14,12},{1,3},{3,1},... | collective-permute-start | bytes 344072 | tf_op jit(solution)/shard_map/ppermute | solution.py:375
  18.9 3.0 %collective-permute-done.2 = bf16[448,128]{1,0:T(8,128)(2,1)S(1)} collective-permute-done((bf16[448,128]{1,0:T(8,128)(2,1)S(1)}, bf16[448,128]{1,0:T(8,128)(2,1)S(1)}, u32[]{:S(2)}, u32[]{:S(2)}) %collective-permute-start.2) | collective-permute-done | bytes 114720 | tf_op jit(solution)/shard_map/ppermute | solution.py:375
  22.0 0.0 copy-start
  22.0 0.1 collective-permute-start.3
  22.1 0.0 copy-done.4
  22.1 0.6 %reshape.11.gain_ref = f32[1,2560]{1,0:T(1,128)} reshape(f32[2560]{0:T(1024)S(1)} %copy-done.4) | data formatting | bytes 20480 | tf_op jit(solution)/shard_map/reshape | solution.py:400
  22.7 2.3 %side.1.side_ref = bf16[320,64]{1,0:T(8,128)(2,1)} custom-call(bf16[64,2560]{1,0:T(8,128)(2,1)} %w_in_ref.1, f32[64,2560]{1,0:T(8,128)} %bitcast.3, f32[1,2560]{1,0:T(1,128)} %reshape.11.gain_ref), custom_call_target="tpu_custom_call" | custom-call | tf_op jit(solution)/shard_map/side/pallas_call | solution.py:422
  25.0 0.0 copy-done
  25.0 0.0 collective-permute-done.3.other_ref
  25.0 0.0 copy-start.2
  25.0 0.7 %copy-done.2 = bf16[896,128]{1,0:T(8,128)(2,1)} copy-done((bf16[896,128]{1,0:T(8,128)(2,1)}, bf16[896,128]{1,0:T(8,128)(2,1)S(1)}, u32[]{:S(2)}) %copy-start.2) | copy-done | bytes 229400
  25.7 5.7 %solve.1 = f32[8,64]{1,0:T(8,128)} custom-call(s32[2,4]{1,0:T(2,128)} %times_ref.1, s32[2]{0:T(128)} %counts_ref.1, f32[8,64]{1,0:T(8,128)} %noise_ref.3, bf16[896,128]{1,0:T(8,128)(2,1)} %copy-done, bf16[896,128]{1,0:T(8,128)(2,1)} %copy-done.2, bf16[320,64]{1,0:T(8,128)(2,1)} %side.1.side_ref), custom_call_target="tpu_custom_call" | custom-call | tf_op jit(solution)/shard_map/solve/pallas_call | solution.py:431
  (2 shorter events, 0.0 us)
Async XLA Ops:
  0.0 1.3 %copy-start.3 = (f32[2560]{0:T(1024)S(1)}, f32[2560]{0:T(1024)}, u32[]{:S(2)}) copy-start(f32[2560]{0:T(1024)} %param.22) | copy-start | bytes 30724
  5.9 11.2 %copy-start.1 = (bf16[112,128]{1,0:T(8,128)(2,1)S(1)}, bf16[112,128]{1,0:T(8,128)(2,1)}, u32[]{:S(2)}) copy-start(bf16[112,128]{1,0:T(8,128)(2,1)} %fold.1) | copy-start | bytes 86020
  5.9 6.3 %collective-permute-start = (bf16[112,128]{1,0:T(8,128)(2,1)}, bf16[112,128]{1,0:T(8,128)(2,1)S(1)}, u32[]{:S(2)}, u32[]{:S(2)}) collective-permute-start(bf16[112,128]{1,0:T(8,128)(2,1)} %fold.1), channel_id=1, source_target_pairs={{0,8},{2,10},{4,12},{6,14},{8,0},{10,2},{12,4},{14,6},{1,9},{3,11}... | collective-permute-start | bytes 86024 | tf_op jit(solution)/shard_map/ppermute | solution.py:375
  12.9 4.2 %collective-permute-start.1 = (bf16[224,128]{1,0:T(8,128)(2,1)S(1)}, bf16[224,128]{1,0:T(8,128)(2,1)S(1)}, u32[]{:S(2)}, u32[]{:S(2)}) collective-permute-start(bf16[224,128]{1,0:T(8,128)(2,1)S(1)} %pad_maximum_fusion.2), channel_id=1, source_target_pairs={{0,4},{2,6},{4,0},{6,2},{8,12},{10,14},{12,8},{14,10},{1,5},{3,7},... | collective-permute-start | bytes 172040 | tf_op jit(solution)/shard_map/ppermute | solution.py:375
  17.1 5.0 %copy-start.4 = (f32[2560]{0:T(1024)S(1)}, f32[2560]{0:T(1024)}, u32[]{:S(2)}) copy-start(f32[2560]{0:T(1024)} %param.23) | copy-start | bytes 30724
  17.1 4.9 %collective-permute-start.2 = (bf16[448,128]{1,0:T(8,128)(2,1)S(1)}, bf16[448,128]{1,0:T(8,128)(2,1)S(1)}, u32[]{:S(2)}, u32[]{:S(2)}) collective-permute-start(bf16[448,128]{1,0:T(8,128)(2,1)S(1)} %pad_maximum_fusion.1), channel_id=1, source_target_pairs={{0,2},{2,0},{4,6},{6,4},{8,10},{10,8},{12,14},{14,12},{1,3},{3,1},... | collective-permute-start | bytes 344072 | tf_op jit(solution)/shard_map/ppermute | solution.py:375
  22.0 3.0 %copy-start = (bf16[896,128]{1,0:T(8,128)(2,1)}, bf16[896,128]{1,0:T(8,128)(2,1)S(1)}, u32[]{:S(2)}) copy-start(bf16[896,128]{1,0:T(8,128)(2,1)S(1)} %pad_maximum_fusion.own_ref) | copy-start | bytes 688132
  22.0 3.0 %collective-permute-start.3 = (bf16[896,128]{1,0:T(8,128)(2,1)S(1)}, bf16[896,128]{1,0:T(8,128)(2,1)S(1)}, u32[]{:S(2)}, u32[]{:S(2)}) collective-permute-start(bf16[896,128]{1,0:T(8,128)(2,1)S(1)} %pad_maximum_fusion.own_ref), channel_id=1, source_target_pairs={{0,1},{1,0},{2,3},{3,2},{4,5},{5,4},{6,7},{7,6},{8,9},{9,8},{10,11... | collective-permute-start | bytes 688136 | tf_op jit(solution)/shard_map/ppermute | solution.py:430
  25.0 0.7 %copy-start.2 = (bf16[896,128]{1,0:T(8,128)(2,1)}, bf16[896,128]{1,0:T(8,128)(2,1)S(1)}, u32[]{:S(2)}) copy-start(bf16[896,128]{1,0:T(8,128)(2,1)S(1)} %collective-permute-done.3.other_ref) | copy-start | bytes 688132

commit v2 on v1

--- a/solution.py
+++ b/solution.py
@@ -81,11 +81,11 @@
 
     def build_lift():
         base = w_in[...].astype(F32)
-        high, low = split2(base * scale_ref[...])
+        high, low = split2(base * scale_ref[...].reshape(1, width))
         lift[0:channels] = w_in[...]
         lift[channels : 2 * channels] = high
         lift[2 * channels : 3 * channels] = low
-        shift_high, shift_low = split2(shift_ref[...])
+        shift_high, shift_low = split2(shift_ref[...].reshape(1, width))
         row = lax.broadcasted_iota(jnp.int32, (16, width), 0)
         tail = jnp.where(
             row == 0,
@@ -210,7 +210,7 @@
     w_in = w_in_ref[...]
     gram = dot(w_in, w_in, NT) * (1.0 / width)
     g_high, g_mid, g_low = split3(gram)
-    gained = w_in.astype(F32) * gain_ref[...]
+    gained = w_in.astype(F32) * gain_ref[...].reshape(1, width)
     s_high, s_low = split2(dot_fine(wf_ref[...], gained))
     out_ref[...] = jnp.concatenate([g_high, g_mid, g_low, s_high, s_low], axis=0)
 
@@ -397,14 +397,13 @@
     count = tokens * heads
     rows = payload_rows(channels)
     wf_t = w_final.T
-    row_of = lambda vector: vector.reshape(1, width)
     vmem = pl.BlockSpec(memory_space=pltpu.VMEM)
     smem = pl.BlockSpec(memory_space=pltpu.SMEM)
     hbm = pl.BlockSpec(memory_space=pl.ANY)
     chunks = 5
     packed = pl.pallas_call(
         functools.partial(fold_kernel, chunks=chunks),
-        out_shape=jax.ShapeDtypeStruct((rows, 2 * channels), BF16),
+        out_shape=pltpu.VMEM((rows, 2 * channels), BF16),
         in_specs=[vmem, hbm, hbm, hbm, hbm, hbm, hbm, vmem, vmem],
         out_specs=vmem,
         scratch_shapes=[
@@ -418,16 +417,20 @@
             pltpu.SemaphoreType.DMA((2 * chunks + 4,)),
         ],
         name="fold",
-    )(noise, w_in, w_query, w_key, w_value, w_out, wf_t, row_of(mod_scale), row_of(mod_shift))
+    )(noise, w_in, w_query, w_key, w_value, w_out, wf_t, mod_scale, mod_shift)
     side = pl.pallas_call(
         side_kernel,
-        out_shape=jax.ShapeDtypeStruct((5 * channels, channels), BF16),
+        out_shape=pltpu.VMEM((5 * channels, channels), BF16),
         in_specs=[vmem, vmem, vmem],
         out_specs=vmem,
         name="side",
-    )(w_in, wf_t, row_of(skip_gain))
+    )(w_in, wf_t, skip_gain)
     own = gathered(packed, "seq")
+    own, side = lax.optimization_barrier((own, side))
     other = lax.ppermute(own, "slab", [(0, 1), (1, 0)])
+    own, other, side = (
+        pltpu.with_memory_space_constraint(value, pltpu.VMEM) for value in (own, other, side)
+    )
     ended = pl.pallas_call(
         functools.partial(solve_kernel, heads=heads),
         out_shape=jax.ShapeDtypeStruct((tokens, channels), F32),

time: 31.7 us -> 25.5 us (0.80)
  local copies, waits for them, and re-layouts: 3.24 us -> 0 us
  Pallas kernels: 11.9 us -> 10.3 us
  other arithmetic: 0.78 us -> 0.03 us
  waiting for transfers between devices: 7.48 us -> 7.07 us
    reshape x3 -> x0, local copies, waits for them, and re-layouts: 2.53 us -> none  [local(): row_of = lambda vector: vector.reshape(1, width)]
    ppermute x3, waiting for transfers between devices: 7.48 us -> 5.59 us  [gathered(): value = jnp.concatenate([value, lax.ppermute(value, axis, pairs)], axis=0)]
    ppermute x1, waiting for transfers between devices: 0.01 us -> 1.48 us  [local(): other = lax.ppermute(own, 'slab', [(0, 1), (1, 0)])]
    pallas_call x2, Pallas kernels: 6.24 us -> 5 us  [the longest x1 3.33 us: local(): pl.pallas_call(functools.partial(fold_kernel, chunks=chunks), out_shape=p...]
    concatenate x3, other arithmetic: 0.78 us -> 0.03 us  [gathered(): value = jnp.concatenate([value, lax.ppermute(value, axis, pairs)], axis=0)]
    unnamed x10 -> x0, local copies, waits for them, and re-layouts: 0.71 us -> none
    pallas_call x1, Pallas kernels: 5.7 us -> 5.25 us  [local(): pl.pallas_call(functools.partial(solve_kernel, heads=heads), out_shape=ja...]
  transfers between devices with their start and end apart: 4 -> 4, of which waited for: 3 -> 4; matrix products, arithmetic and copies ran while one was open for 2% -> 0% of each run, Pallas kernels for 7% -> 7%
where the time goes in v2:
time: 25.5 us; the launch traced here: 25.3 us
  Pallas kernels  10.3 us (40%)
  starting transfers between devices  7.88 us (31%)
  waiting for transfers between devices  7.07 us (28%)
    ppermute x3, starting transfers between devices, gathered(): value = jnp.concatenate([value, lax.ppermute(value, axis, pairs)], axis=0)  7.81 us
    ppermute x3, waiting for transfers between devices, gathered(): value = jnp.concatenate([value, lax.ppermute(value, axis, pairs)], axis=0)  5.59 us
    pallas_call x1, Pallas kernels, local(): pl.pallas_call(functools.partial(solve_kernel, heads=heads), out_shape=ja...  5.25 us
    pallas_call x1, Pallas kernels, local(): pl.pallas_call(functools.partial(fold_kernel, chunks=chunks), out_shape=p...  3.33 us
    pallas_call x1, Pallas kernels, local(): pl.pallas_call(side_kernel, out_shape=pltpu.VMEM((5 * channels, channels)...  1.68 us
    ppermute x1, waiting for transfers between devices, local(): other = lax.ppermute(own, 'slab', [(0, 1), (1, 0)])  1.48 us
  transfers between devices with their start and end apart: 4, of which 4 were waited for; matrix products, arithmetic and copies ran while one was open for 0% of the time, Pallas kernels for 7%

profile of v2, /device:TPU:0, one launch (start us, length us, event | category | flops | bytes accessed | tf_op | source)
XLA Modules:
  0.0 25.3 jit_solution(14244159698349704955)
XLA Ops:
  0.0 3.3 %fold.1 = bf16[112,128]{1,0:T(8,128)(2,1)S(1)} custom-call(f32[8,64]{1,0:T(8,128)} %noise_ref.3, bf16[64,2560]{1,0:T(8,128)(2,1)} %w_in_ref.1, bf16[2560,128]{1,0:T(8,128)(2,1)} %wq_hbm.1, bf16[2560,128]{1,0:T(8,128)(2,1)} %wk_hbm.1, bf16[2560,128]{1,0:T(8,128)(2,1)} %wv_hbm.1, bf16[128,2560]{1,0:T(8,128)(2,1)} %wo_hbm.1, f32[64,2560]{1,0:T(8,128)} %bitcast.2, ...), custom_call_target="tpu_custom_call" | custom-call | tf_op jit(solution)/shard_map/fold/pallas_call | solution.py:404
  3.3 4.1 %collective-permute-start = (bf16[112,128]{1,0:T(8,128)(2,1)S(1)}, bf16[112,128]{1,0:T(8,128)(2,1)S(1)}, u32[]{:S(2)}, u32[]{:S(2)}) collective-permute-start(bf16[112,128]{1,0:T(8,128)(2,1)S(1)} %fold.1), channel_id=1, source_target_pairs={{0,8},{2,10},{4,12},{6,14},{8,0},{10,2},{12,4},{14,6},{1,9},{3,11}... | collective-permute-start | bytes 86024 | tf_op jit(solution)/shard_map/ppermute | solution.py:375
  7.5 1.9 %collective-permute-done = bf16[112,128]{1,0:T(8,128)(2,1)S(1)} collective-permute-done((bf16[112,128]{1,0:T(8,128)(2,1)S(1)}, bf16[112,128]{1,0:T(8,128)(2,1)S(1)}, u32[]{:S(2)}, u32[]{:S(2)}) %collective-permute-start) | collective-permute-done | bytes 28704 | tf_op jit(solution)/shard_map/ppermute | solution.py:375
  9.4 1.8 %collective-permute-start.1 = (bf16[224,128]{1,0:T(8,128)(2,1)S(1)}, bf16[224,128]{1,0:T(8,128)(2,1)S(1)}, u32[]{:S(2)}, u32[]{:S(2)}) collective-permute-start(bf16[224,128]{1,0:T(8,128)(2,1)S(1)} %pad_maximum_fusion.2), channel_id=1, source_target_pairs={{0,4},{2,6},{4,0},{6,2},{8,12},{10,14},{12,8},{14,10},{1,5},{3,7},... | collective-permute-start | bytes 172040 | tf_op jit(solution)/shard_map/ppermute | solution.py:375
  11.2 2.3 %collective-permute-done.1 = bf16[224,128]{1,0:T(8,128)(2,1)S(1)} collective-permute-done((bf16[224,128]{1,0:T(8,128)(2,1)S(1)}, bf16[224,128]{1,0:T(8,128)(2,1)S(1)}, u32[]{:S(2)}, u32[]{:S(2)}) %collective-permute-start.1) | collective-permute-done | bytes 57376 | tf_op jit(solution)/shard_map/ppermute | solution.py:375
  13.6 1.8 %collective-permute-start.2 = (bf16[448,128]{1,0:T(8,128)(2,1)S(1)}, bf16[448,128]{1,0:T(8,128)(2,1)S(1)}, u32[]{:S(2)}, u32[]{:S(2)}) collective-permute-start(bf16[448,128]{1,0:T(8,128)(2,1)S(1)} %pad_maximum_fusion.1), channel_id=1, source_target_pairs={{0,2},{2,0},{4,6},{6,4},{8,10},{10,8},{12,14},{14,12},{1,3},{3,1},... | collective-permute-start | bytes 344072 | tf_op jit(solution)/shard_map/ppermute | solution.py:375
  15.4 1.7 %side.1.side_ref = bf16[320,64]{1,0:T(8,128)(2,1)S(1)} custom-call(bf16[64,2560]{1,0:T(8,128)(2,1)} %w_in_ref.1, f32[64,2560]{1,0:T(8,128)} %bitcast.3, f32[2560]{0:T(1024)} %gain_ref.1), custom_call_target="tpu_custom_call" | custom-call | tf_op jit(solution)/shard_map/side/pallas_call | solution.py:421
  17.1 1.3 %collective-permute-done.2 = bf16[448,128]{1,0:T(8,128)(2,1)S(1)} collective-permute-done((bf16[448,128]{1,0:T(8,128)(2,1)S(1)}, bf16[448,128]{1,0:T(8,128)(2,1)S(1)}, u32[]{:S(2)}, u32[]{:S(2)}) %collective-permute-start.2) | collective-permute-done | bytes 114720 | tf_op jit(solution)/shard_map/ppermute | solution.py:375
  18.5 0.1 collective-permute-start.3
  18.5 1.5 %collective-permute-done.3.other_ref = bf16[896,128]{1,0:T(8,128)(2,1)S(1)} collective-permute-done((bf16[896,128]{1,0:T(8,128)(2,1)S(1)}, bf16[896,128]{1,0:T(8,128)(2,1)S(1)}, u32[]{:S(2)}, u32[]{:S(2)}) %collective-permute-start.3) | collective-permute-done | bytes 229408 | tf_op jit(solution)/shard_map/ppermute | solution.py:430
  20.0 5.2 %solve.1 = f32[8,64]{1,0:T(8,128)} custom-call(s32[2,4]{1,0:T(2,128)} %times_ref.1, s32[2]{0:T(128)} %counts_ref.1, f32[8,64]{1,0:T(8,128)} %noise_ref.3, bf16[896,128]{1,0:T(8,128)(2,1)S(1)} %pad_maximum_fusion.own_ref, bf16[896,128]{1,0:T(8,128)(2,1)S(1)} %collective-permute-done.3.other_ref, bf16[320,64]{1,0:T(8,128)(2,1)S(1)} %side.1.side_ref), custom_call_target="tpu_custom_call" | custom-call | tf_op jit(solution)/shard_map/solve/pallas_call | solution.py:434
  (3 shorter events, 0.0 us)
Async XLA Ops:
  3.3 6.1 %collective-permute-start = (bf16[112,128]{1,0:T(8,128)(2,1)S(1)}, bf16[112,128]{1,0:T(8,128)(2,1)S(1)}, u32[]{:S(2)}, u32[]{:S(2)}) collective-permute-start(bf16[112,128]{1,0:T(8,128)(2,1)S(1)} %fold.1), channel_id=1, source_target_pairs={{0,8},{2,10},{4,12},{6,14},{8,0},{10,2},{12,4},{14,6},{1,9},{3,11}... | collective-permute-start | bytes 86024 | tf_op jit(solution)/shard_map/ppermute | solution.py:375
  9.4 4.2 %collective-permute-start.1 = (bf16[224,128]{1,0:T(8,128)(2,1)S(1)}, bf16[224,128]{1,0:T(8,128)(2,1)S(1)}, u32[]{:S(2)}, u32[]{:S(2)}) collective-permute-start(bf16[224,128]{1,0:T(8,128)(2,1)S(1)} %pad_maximum_fusion.2), channel_id=1, source_target_pairs={{0,4},{2,6},{4,0},{6,2},{8,12},{10,14},{12,8},{14,10},{1,5},{3,7},... | collective-permute-start | bytes 172040 | tf_op jit(solution)/shard_map/ppermute | solution.py:375
  13.6 4.9 %collective-permute-start.2 = (bf16[448,128]{1,0:T(8,128)(2,1)S(1)}, bf16[448,128]{1,0:T(8,128)(2,1)S(1)}, u32[]{:S(2)}, u32[]{:S(2)}) collective-permute-start(bf16[448,128]{1,0:T(8,128)(2,1)S(1)} %pad_maximum_fusion.1), channel_id=1, source_target_pairs={{0,2},{2,0},{4,6},{6,4},{8,10},{10,8},{12,14},{14,12},{1,3},{3,1},... | collective-permute-start | bytes 344072 | tf_op jit(solution)/shard_map/ppermute | solution.py:375
  18.5 1.6 %collective-permute-start.3 = (bf16[896,128]{1,0:T(8,128)(2,1)S(1)}, bf16[896,128]{1,0:T(8,128)(2,1)S(1)}, u32[]{:S(2)}, u32[]{:S(2)}) collective-permute-start(bf16[896,128]{1,0:T(8,128)(2,1)S(1)} %pad_maximum_fusion.own_ref), channel_id=1, source_target_pairs={{0,1},{1,0},{2,3},{3,2},{4,5},{5,4},{6,7},{7,6},{8,9},{9,8},{10,11... | collective-permute-start | bytes 688136 | tf_op jit(solution)/shard_map/ppermute | solution.py:430

commit v3 on v0

v3 whole, which is shorter than its diff:
```python
import functools
import math

import jax
import jax.numpy as jnp
from jax import lax
from jax.experimental import pallas as pl
from jax.experimental.pallas import tpu as pltpu
from jax.sharding import PartitionSpec as P

HEAD_SIZE = 128
F32 = jnp.float32
BF16 = jnp.bfloat16
NT = (((1,), (1,)), ((), ()))
TN = (((0,), (0,)), ((), ()))


def dot(a, b, dims=(((1,), (0,)), ((), ()))):
    return lax.dot_general(a, b, dims, preferred_element_type=F32)


def split2(x):
    high = x.astype(BF16)
    return high, (x - high.astype(F32)).astype(BF16)


def split3(x):
    high = x.astype(BF16)
    mid, low = split2(x - high.astype(F32))
    return high, mid, low


def dot_fine(a, b):
    a_high, a_low = split2(a)
    b_high, b_low = split2(b)
    return dot(
        jnp.concatenate([a_high, a_high, a_low], axis=1),
        jnp.concatenate([b_high, b_low, b_high], axis=1),
        NT,
    )


def layout(channels, tokens):
    second = channels
    third = second + channels // 2
    tail = third + channels
    return second, third, tail, tail + 4 + tokens // 2 + tokens


def iotas(rows, columns):
    return (
        lax.broadcasted_iota(jnp.int32, (rows, columns), 0),
        lax.broadcasted_iota(jnp.int32, (rows, columns), 1),
    )


def fold_kernel(
    noise_ref,
    w_in_hbm,
    wq_hbm,
    wk_hbm,
    wv_hbm,
    wo_hbm,
    wf_hbm,
    scale_ref,
    shift_ref,
    out_ref,
    w_in,
    lift,
    w_a,
    w_b,
    w_c,
    wo,
    wf,
    wf2,
    sems,
    *,
    chunks,
):
    slab = lax.axis_index("slab")
    channels, width = w_in.shape
    depth = width // chunks
    half = channels // 2
    tokens = noise_ref.shape[0]
    second, third, tail, rows_all = layout(channels, tokens)

    def fetch(src, dst, index):
        copy = pltpu.make_async_copy(src, dst, sems.at[index])
        copy.start()
        return copy

    def parts(total):
        last = total[3 * channels : 3 * channels + 8]
        return (
            total[0:channels],
            total[channels : 2 * channels] + total[2 * channels : 3 * channels],
            last[0:1] + last[1:2],
        )

    @pl.when(slab == 0)
    def _():
        out_ref[...] = jnp.zeros_like(out_ref)

    @pl.when(slab != 0)
    def _():
        first = fetch(w_in_hbm, w_in, 0)
        copies = []
        for c in range(chunks):
            at = pl.ds(c * depth, depth)
            copies.append(
                [
                    fetch(src.at[at], dst.at[at], 3 + 3 * c + i)
                    for i, (src, dst) in enumerate(((wq_hbm, w_a), (wk_hbm, w_b), (wv_hbm, w_c)))
                ]
            )
        final_copy = fetch(wf_hbm, wf, 1)
        out_copy = fetch(wo_hbm, wo, 2)
        shift_high, shift_low = split2(shift_ref[...].reshape(1, width))
        row, _ = iotas(16, width)
        lift[3 * channels : 3 * channels + 16] = jnp.where(
            row == 0,
            shift_high.astype(F32),
            jnp.where(row == 1, shift_low.astype(F32), 0.0),
        ).astype(BF16)
        scale = scale_ref[...].reshape(1, width)
        first.wait()
        lift[0:channels] = w_in[...]
        high, low = split2(w_in[...].astype(F32) * scale)
        lift[channels : 2 * channels] = high
        lift[2 * channels : 3 * channels] = low
        total = None
        for c in range(chunks):
            at = slice(c * depth, (c + 1) * depth)
            for copy in copies[c]:
                copy.wait()
            term = dot(lift[:, at], jnp.concatenate([w_a[at], w_b[at], w_c[at]], axis=1))
            total = term if total is None else total + term
        final_copy.wait()
        high, low = split2(wf[...])
        wf2[0:channels] = high
        wf2[channels : 2 * channels] = low
        out_copy.wait()
        both = dot(wf2[...], wo[...], NT)
        out_t = both[0:channels] + both[channels : 2 * channels]
        q0, q1, q2 = parts(total[:, 0:HEAD_SIZE] * (math.log2(math.e) / math.sqrt(HEAD_SIZE)))
        k0, k1, k2 = parts(total[:, HEAD_SIZE : 2 * HEAD_SIZE])
        v0, v1, v2 = parts(total[:, 2 * HEAD_SIZE : 3 * HEAD_SIZE])
        pad = jnp.zeros((7, HEAD_SIZE), F32)
        q_all = jnp.concatenate([q0, q1], axis=0)
        k_all = jnp.concatenate([k0, k1], axis=0)
        form = dot_fine(k_all, q_all)
        a_rows = dot_fine(jnp.concatenate([k2, pad], axis=0), q_all)
        b_rows = dot_fine(jnp.concatenate([q2, pad], axis=0), k_all)
        constant = jnp.sum(k2 * q2)
        p_rows = dot_fine(
            jnp.concatenate([v2, pad], axis=0), jnp.concatenate([out_t, out_t], axis=0)
        )
        _, lane = iotas(channels, 2 * channels)
        top, bottom = form[0:channels], form[channels : 2 * channels]
        rolled = pltpu.roll(bottom, channels, 1)
        out_ref[0:channels] = jnp.where(lane < channels, top, top + rolled).astype(BF16)
        out_ref[second:third] = jnp.where(
            lane[0:half] < channels, rolled[0:half], bottom[half:channels]
        ).astype(BF16)
        out_ref[third:tail] = dot_fine(out_t, jnp.concatenate([v0, v1], axis=0)).astype(BF16)
        n_high, n_mid, n_low = (part.astype(F32) for part in split3(noise_ref[...]))
        lows = jnp.concatenate([n_low[0 : tokens // 2], n_low[tokens // 2 : tokens]], axis=1)
        row, lane = iotas(4, 2 * channels)
        left = lane < channels
        a_roll = pltpu.roll(a_rows, channels, 1)[0:1]
        b_roll = pltpu.roll(b_rows, channels, 1)[0:1]
        at_const = (lane == channels + 2) | (lane == channels + 3)
        vectors = jnp.where(
            row == 0,
            jnp.where(left, 0.0, a_roll),
            jnp.where(
                row == 1,
                jnp.where(left, a_roll, jnp.where(at_const, constant, 0.0)),
                jnp.where(row == 2, jnp.where(left, b_rows[0:1], p_rows[0:1]), b_roll),
            ),
        )
        out_ref[tail:rows_all] = jnp.concatenate(
            [vectors, lows, jnp.concatenate([n_high, n_mid], axis=1)], axis=0
        ).astype(BF16)


def unpack(pay_ref, base, h, t2, t2z, a1, a2, start, channels, tokens):
    second, third, tail, rows_all = layout(channels, tokens)
    folded = pay_ref[pl.ds(base + second, third - second)]
    ext = pay_ref[pl.ds(base + tail, rows_all - tail)]
    _, wide = iotas(channels, 2 * channels)
    row, lane = iotas(rows_all - tail, 2 * channels)
    lane = lane - channels
    b_pick = ((row == 2) & ((lane == 0) | (lane == 1))) | (
        (row == 3) & ((lane == 2) | (lane == 3))
    )
    p_pick = (row == 2) & ((lane == 4) | (lane == 5))
    ones = jnp.ones(row.shape, F32)
    folded = folded.astype(F32)
    ext = ext.astype(F32)
    b_side = jnp.transpose(ext)
    columns = dot(b_side[0:channels].astype(BF16), jnp.where(b_pick, ones, 0.0).astype(BF16))
    p_columns = dot(
        b_side[channels : 2 * channels].astype(BF16), jnp.where(p_pick, ones, 0.0).astype(BF16)
    )
    square = jnp.concatenate([folded, pltpu.roll(folded, channels, 1)], axis=0)
    at = pl.ds(h * channels, channels)
    t2[at] = jnp.where(wide < channels, square, columns).astype(BF16)
    t2z[at] = p_columns.astype(BF16)
    a1[pl.ds(h, 1)] = ext[0:1]
    a2[pl.ds(h, 1)] = ext[1:2]
    lows = ext[4 : 4 + tokens // 2]
    pieces = ext[4 + tokens // 2 :]
    low = jnp.concatenate([lows, pltpu.roll(lows, channels, 1)], axis=0)
    whole = (pieces + pltpu.roll(pieces, channels, 1)) + low
    start[pl.ds(h * tokens, tokens)] = whole


def side_kernel(
    times_ref,
    counts_ref,
    w_in_ref,
    wf_ref,
    gain_ref,
    pay_ref,
    out_ref,
    plan_ref,
    t2,
    t2z,
    a1,
    a2,
    start,
    *,
    heads,
    rows_all,
    tokens,
):
    channels, width = w_in_ref.shape
    w_in = w_in_ref[...]
    gram = dot(w_in, w_in, NT) * (1.0 / width)
    gained = w_in.astype(F32) * gain_ref[...].reshape(1, width)
    skip = dot_fine(wf_ref[...], gained)
    for h in range(heads):
        unpack(pay_ref, h * rows_all, h, t2, t2z, a1, a2, start, channels, tokens)
    g_high, g_mid, g_low = split3(gram)
    s_high, s_low = split2(skip)
    out_ref[...] = jnp.concatenate([g_high, g_mid, g_low, s_high, s_low], axis=0)

    lanes = plan_ref.shape[1]
    points = times_ref.shape[1]

    def level(slab_id, column):
        whole = jnp.zeros((1, lanes), jnp.int32) + times_ref[slab_id, column]
        return whole.astype(F32) / 1000.0

    for k in range(2):
        levels = [level(k, column) for column in range(points)]
        last = jnp.zeros((1, lanes), F32)
        for column in range(points):
            last = jnp.where(column == counts_ref[k], levels[column], last)
        steps = [
            jnp.where(j < counts_ref[k], levels[j + 1] - levels[j], 0.0)
            for j in range(points - 1)
        ]
        rows = levels + steps + [last - levels[0]]
        for i, value in enumerate(rows):
            plan_ref[pl.ds(k * 2 * points + i, 1)] = value


def solve_kernel(
    pay_ref,
    side_ref,
    plan_ref,
    t2h_ref,
    t2zh_ref,
    a1h_ref,
    a2h_ref,
    starth_ref,
    before_ref,
    out_ref,
    t2,
    t2z,
    a1,
    a2,
    start,
    *,
    heads,
    tokens,
    slab_id,
    ready,
    points,
):
    slab = lax.axis_index("slab")
    channels = side_ref.shape[1]
    count = heads * tokens
    lanes = 2 * count
    second, third, tail, rows_all = layout(channels, tokens)
    fine_most = points - 1

    @pl.when(slab != slab_id)
    def _():
        out_ref[...] = before_ref[...]

    @pl.when(slab == slab_id)
    def _():
        for h in range(ready, heads):
            unpack(pay_ref, h * rows_all, h, t2, t2z, a1, a2, start, channels, tokens)
        if ready:
            for dst, src in (
                (a1, a1h_ref),
                (a2, a2h_ref),
                (start, starth_ref),
            ):
                dst[0 : src.shape[0]] = src[...]

        def from_half(h, dst, src):
            at = slice(h * channels, (h + 1) * channels)
            return src[at] if h < ready else dst[at]

        _, lane = iotas(1, lanes)
        left = lane < count

        def level(k, column):
            return plan_ref[k * 2 * points + column : k * 2 * points + column + 1]

        def step(k, j):
            return level(k, points + j)

        def span(k):
            return level(k, 2 * points - 1)

        def velocity(u, s):
            rounded = u.astype(BF16)
            sides = dot(side_ref[...], rounded)
            form = (
                sides[0:channels] + sides[channels : 2 * channels]
            ) + sides[2 * channels : 3 * channels]
            squares = jnp.sum(form * rounded.astype(F32), axis=0, keepdims=True)
            r = lax.rsqrt(jnp.maximum(squares, 0.0) + 1e-06)
            skip = r * (sides[3 * channels : 4 * channels] + sides[4 * channels : 5 * channels])
            s2 = s * s
            s_high, s_low = (part.astype(F32) for part in split2(s))
            s2_high, s2_low = (part.astype(F32) for part in split2(s2))
            row, _ = iotas(channels, lanes)
            s_rows = jnp.zeros((channels, lanes), F32)
            for i, value in enumerate((s_high, s_low, s2_high, s2_low, s_high, s_low)):
                s_rows = jnp.where(row == i, value, s_rows)
            x = r * rounded.astype(F32)
            features = jnp.concatenate(
                [x.astype(BF16), (s * x).astype(BF16), (s2 * x).astype(BF16), s_rows.astype(BF16)],
                axis=0,
            )
            keys = jnp.transpose(x)
            keys = jnp.concatenate([keys[0:count], keys[count:lanes]], axis=1).astype(BF16)
            maps = []
            for h in range(heads):
                base = h * rows_all
                maps.append(
                    jnp.concatenate(
                        [pay_ref[base : base + channels], from_half(h, t2, t2h_ref)], axis=1
                    )
                )
            queries = dot(jnp.concatenate(maps, axis=0), features)
            offsets = dot(
                jnp.concatenate([a1[...], a2[...]], axis=1).astype(BF16), features
            )
            maps = []
            for h in range(heads):
                base = h * rows_all
                maps.append(
                    jnp.concatenate(
                        [pay_ref[base + third : base + tail], from_half(h, t2z, t2zh_ref)], axis=1
                    )
                )
            values = dot(jnp.concatenate(maps, axis=0), features).astype(BF16)
            lhs, rhs = [], []
            for h in range(heads):
                at = slice(h * channels, (h + 1) * channels)
                query = queries[at]
                both = jnp.concatenate(
                    [jnp.where(left, query, 0.0), jnp.where(left, 0.0, query)], axis=0
                )
                scores = dot(keys, both.astype(BF16)) + offsets[h : h + 1]
                raised = jnp.exp2(scores - jnp.max(scores, axis=0, keepdims=True))
                weights = raised / jnp.sum(raised, axis=0, keepdims=True)
                lhs.append(values[at])
                rhs.append(jnp.where(left, weights, 0.0).astype(BF16))
                rhs.append(jnp.where(left, 0.0, weights).astype(BF16))
            return skip + dot(jnp.concatenate(lhs, axis=1), jnp.concatenate(rhs, axis=0))

        noise = jnp.transpose(start[...])[0:channels]
        noise = jnp.concatenate([noise, noise], axis=1)
        moved = velocity(noise, level(0, 0))
        first_coarse = noise + span(0) * moved
        if slab_id == 0:
            u = noise + step(0, 0) * moved
            for j in range(1, fine_most):
                u = u + step(0, j) * velocity(u, level(0, j))
            ended = first_coarse + (u - first_coarse)
        else:
            u = jnp.where(left, noise + step(0, 0) * moved, first_coarse)
            coarse_old = None
            for j in range(fine_most):
                last = j == fine_most - 1
                s = jnp.where(left, level(1, 0) if last else level(0, j + 1), level(1, j))
                moved = velocity(u, s)
                if j == 0:
                    coarse_old = u + span(1) * moved
                u = u + jnp.where(left, span(1) if last else step(0, j + 1), step(1, j)) * moved
            ended = u + pltpu.roll(u - coarse_old, count, 1)
        out_ref[...] = jnp.transpose(ended)[0:tokens, 0:channels]


def exchanged(value, stride):
    groups, size, slabs = (lax.axis_size(axis) for axis in ("groups", "seq", "slab"))
    pairs = []
    for g in range(groups):
        for s in range(size):
            for c in range(slabs):
                if c == slabs - 1 or groups % 2:
                    to = (g, s ^ stride)
                else:
                    to = (g ^ 1, s)
                pairs.append(((g * size + s) * slabs + c, (to[0] * size + to[1]) * slabs + c))
    return lax.ppermute(value, ("groups", "seq", "slab"), pairs)


def local(
    noise,
    timesteps,
    fine_counts,
    w_in,
    w_query,
    w_key,
    w_value,
    w_out,
    w_final,
    mod_scale,
    mod_shift,
    skip_gain,
):
    channels, width = w_in.shape
    tokens = noise.shape[0]
    heads = lax.axis_size("seq")
    half = heads // 2
    count = tokens * heads
    points = timesteps.shape[1]
    *_, rows = layout(channels, tokens)
    wf_t = w_final.T
    vmem = pl.BlockSpec(memory_space=pltpu.VMEM)
    smem = pl.BlockSpec(memory_space=pltpu.SMEM)
    hbm = pl.BlockSpec(memory_space=pl.ANY)
    chunks = 5

    def near(*values):
        return [pltpu.with_memory_space_constraint(value, pltpu.VMEM) for value in values]

    packed = pl.pallas_call(
        functools.partial(fold_kernel, chunks=chunks),
        out_shape=pltpu.VMEM((rows, 2 * channels), BF16),
        in_specs=[vmem, hbm, hbm, hbm, hbm, hbm, hbm, vmem, vmem],
        out_specs=vmem,
        scratch_shapes=[
            pltpu.VMEM((channels, width), BF16),
            pltpu.VMEM((3 * channels + 16, width), BF16),
            pltpu.VMEM((width, HEAD_SIZE), BF16),
            pltpu.VMEM((width, HEAD_SIZE), BF16),
            pltpu.VMEM((width, HEAD_SIZE), BF16),
            pltpu.VMEM((HEAD_SIZE, width), BF16),
            pltpu.VMEM((channels, width), F32),
            pltpu.VMEM((2 * channels, width), BF16),
            pltpu.SemaphoreType.DMA((3 * chunks + 3,)),
        ],
        name="fold",
    )(noise, w_in, w_query, w_key, w_value, w_out, wf_t, mod_scale, mod_shift)
    stride = half
    own = packed
    while stride > 1:
        own = jnp.concatenate([own, exchanged(own, stride)], axis=0)
        stride //= 2

    def tables(n, kind):
        return (
            kind((n * channels, 2 * channels), BF16),
            kind((n * channels, 2 * channels), BF16),
            kind((n, 2 * channels), F32),
            kind((n, 2 * channels), F32),
            kind((n * tokens, 2 * channels), F32),
        )

    side, plan, *firsts = pl.pallas_call(
        functools.partial(side_kernel, heads=half, rows_all=rows, tokens=tokens),
        out_shape=(
            pltpu.VMEM((5 * channels, channels), BF16),
            pltpu.VMEM((4 * points, 2 * count), F32),
            *tables(half, pltpu.VMEM),
        ),
        in_specs=[smem, smem, vmem, vmem, vmem, vmem],
        out_specs=(vmem,) * 7,
        name="side",
    )(timesteps, fine_counts, w_in, wf_t, skip_gain, *near(own))
    own = jnp.concatenate([own, exchanged(own, 1)], axis=0)
    own, side, plan, *firsts = lax.optimization_barrier((own, side, plan, *firsts))
    other = lax.ppermute(own, "slab", [(0, 1), (1, 0)])

    def solve(slab_id, pay, before, kind):
        return pl.pallas_call(
            functools.partial(
                solve_kernel,
                heads=heads,
                tokens=tokens,
                slab_id=slab_id,
                ready=half if slab_id else 0,
                points=points,
            ),
            out_shape=kind((tokens, channels), F32),
            in_specs=[vmem] * 9,
            out_specs=vmem,
            scratch_shapes=tables(heads, pltpu.VMEM),
            name=f"solve{slab_id}",
        )(*near(pay, side, plan, *firsts, before))

    ended = solve(1, own, plan[0:tokens, 0:channels], pltpu.VMEM)
    ended = solve(0, other, ended, jax.ShapeDtypeStruct)
    return ended[None]


def solution(mesh):
    placed = (
        P(("groups", "seq"), None),
        P("groups", None),
        P("groups"),
        P(),
        P(None, "seq"),
        P(None, "seq"),
        P(None, "seq"),
        P("seq", None),
        P(),
        P(),
        P(),
        P(),
    )
    return jax.shard_map(
        local,
        mesh=mesh,
        in_specs=placed,
        out_specs=P("slab", ("groups", "seq"), None),
        check_vma=False,
    )
```

time: 361 us -> 22.1 us (0.06)
  blocking collectives: 325 us -> 0 us
  matrix products: 14 us -> 0 us
  between operations: 7.77 us -> 0.03 us
  waiting for transfers between devices: 0.81 us -> 7.58 us
  Pallas kernels: 0 us -> 5.92 us
  starting transfers between devices: 2.58 us -> 8.25 us
  other arithmetic: 5.2 us -> 0.04 us
  local copies, waits for them, and re-layouts: 4.82 us -> 0.01 us
    unnamed x5 -> x0, blocking collectives: 169 us -> none
    all_gather x5 -> x0, blocking collectives: 156 us -> none  [velocity(): lax.all_gather(modulated, 'seq', axis=0, tiled=True)]
    dot_general x31 -> x0, matrix products: 14 us -> none  [the longest x5 4 us: velocity(): jnp.dot(skip_gain * normed, w_final, precision=lax.Precision.HIGHEST, pre...]
    ppermute x2 -> x4, waiting for transfers between devices: 0.81 us -> 7.58 us  [the longest x3 6.28 us: exchanged(): return lax.ppermute(value, ('groups', 'seq', 'slab'), pairs)]
    pallas_call x0 -> x4, Pallas kernels: none -> 5.92 us  [the longest x2 3.3 us: solve(): pl.pallas_call(functools.partial(solve_kernel, heads=heads, tokens=tokens...]
    ppermute x2 -> x4, starting transfers between devices: 2.58 us -> 8.25 us  [the longest x3 7.2 us: exchanged(): return lax.ppermute(value, ('groups', 'seq', 'slab'), pairs)]
  transfers between devices with their start and end apart: 2 -> 4, of which waited for: 1 -> 4; matrix products, arithmetic and copies ran while one was open for 0% -> 0% of each run, Pallas kernels for 0% -> 8%
where the time goes in v3:
time: 22.1 us; the launch traced here: 21.8 us
  starting transfers between devices  8.25 us (37%)
  waiting for transfers between devices  7.58 us (34%)
  Pallas kernels  5.92 us (27%)
    ppermute x3, starting transfers between devices, exchanged(): return lax.ppermute(value, ('groups', 'seq', 'slab'), pairs)  7.2 us
    ppermute x3, waiting for transfers between devices, exchanged(): return lax.ppermute(value, ('groups', 'seq', 'slab'), pairs)  6.28 us
    pallas_call x2, Pallas kernels, solve(): pl.pallas_call(functools.partial(solve_kernel, heads=heads, tokens=tokens...  3.3 us
    pallas_call x1, Pallas kernels, local(): pl.pallas_call(functools.partial(side_kernel, heads=half, rows_all=rows,...  1.72 us
    ppermute x1, waiting for transfers between devices, local(): other = lax.ppermute(own, 'slab', [(0, 1), (1, 0)])  1.29 us
    ppermute x1, starting transfers between devices, local(): other = lax.ppermute(own, 'slab', [(0, 1), (1, 0)])  1.05 us
    pallas_call x1, Pallas kernels, local(): pl.pallas_call(functools.partial(fold_kernel, chunks=chunks), out_shape=p...  0.9 us
  transfers between devices with their start and end apart: 4, of which 4 were waited for; matrix products, arithmetic and copies ran while one was open for 0% of the time, Pallas kernels for 8%

profile of v3, /device:TPU:0, one launch (start us, length us, event | category | flops | bytes accessed | tf_op | source)
XLA Modules:
  0.0 21.8 jit_solution(688367922563855705)
XLA Ops:
  0.0 0.9 %fold.1 = bf16[176,128]{1,0:T(8,128)(2,1)S(1)} custom-call(f32[8,64]{1,0:T(8,128)} %noise_ref.1, bf16[64,2560]{1,0:T(8,128)(2,1)} %w_in_ref.1, bf16[2560,128]{1,0:T(8,128)(2,1)} %wq_hbm.1, bf16[2560,128]{1,0:T(8,128)(2,1)} %wk_hbm.1, bf16[2560,128]{1,0:T(8,128)(2,1)} %wv_hbm.1, bf16[128,2560]{1,0:T(8,128)(2,1)} %wo_hbm.1, f32[64,2560]{1,0:T(8,128)} %bitcast.2, ...), custom_call_target="tpu_custom_call" | custom-call | tf_op jit(solution)/shard_map/fold/pallas_call | solution.py:458
  0.9 3.0 %collective-permute-start = (bf16[176,128]{1,0:T(8,128)(2,1)S(1)}, bf16[176,128]{1,0:T(8,128)(2,1)S(1)}, u32[]{:S(2)}, u32[]{:S(2)}) collective-permute-start(bf16[176,128]{1,0:T(8,128)(2,1)S(1)} %fold.1), channel_id=1, source_target_pairs={{0,16},{1,9},{2,18},{3,11},{4,20},{5,13},{6,22},{7,15},{8,24},{9,1... | collective-permute-start | bytes 135176 | tf_op jit(solution)/shard_map/ppermute | solution.py:425
  3.9 2.0 %collective-permute-done = bf16[176,128]{1,0:T(8,128)(2,1)S(1)} collective-permute-done((bf16[176,128]{1,0:T(8,128)(2,1)S(1)}, bf16[176,128]{1,0:T(8,128)(2,1)S(1)}, u32[]{:S(2)}, u32[]{:S(2)}) %collective-permute-start) | collective-permute-done | bytes 45088 | tf_op jit(solution)/shard_map/ppermute | solution.py:425
  6.0 2.1 %collective-permute-start.1 = (bf16[352,128]{1,0:T(8,128)(2,1)S(1)}, bf16[352,128]{1,0:T(8,128)(2,1)S(1)}, u32[]{:S(2)}, u32[]{:S(2)}) collective-permute-start(bf16[352,128]{1,0:T(8,128)(2,1)S(1)} %pad_maximum_fusion.2), channel_id=1, source_target_pairs={{0,16},{1,5},{2,18},{3,7},{4,20},{5,1},{6,22},{7,3},{8,24},{9,13},... | collective-permute-start | bytes 270344 | tf_op jit(solution)/shard_map/ppermute | solution.py:425
  8.1 2.5 %collective-permute-done.1 = bf16[352,128]{1,0:T(8,128)(2,1)S(1)} collective-permute-done((bf16[352,128]{1,0:T(8,128)(2,1)S(1)}, bf16[352,128]{1,0:T(8,128)(2,1)S(1)}, u32[]{:S(2)}, u32[]{:S(2)}) %collective-permute-start.1) | collective-permute-done | bytes 90144 | tf_op jit(solution)/shard_map/ppermute | solution.py:425
  10.6 2.1 %collective-permute-start.2 = (bf16[704,128]{1,0:T(8,128)(2,1)S(1)}, bf16[704,128]{1,0:T(8,128)(2,1)S(1)}, u32[]{:S(2)}, u32[]{:S(2)}) collective-permute-start(bf16[704,128]{1,0:T(8,128)(2,1)S(1)} %pad_maximum_fusion.1.pay_ref), channel_id=1, source_target_pairs={{0,16},{1,3},{2,18},{3,1},{4,20},{5,7},{6,22},{7,5},{8,24},{9,11},... | collective-permute-start | bytes 540680 | tf_op jit(solution)/shard_map/ppermute | solution.py:425
  12.7 1.7 %side.1 = (bf16[320,64]{1,0:T(8,128)(2,1)S(1)}, f32[16,128]{1,0:T(8,128)S(1)}, bf16[256,128]{1,0:T(8,128)(2,1)S(1)}, bf16[256,128]{1,0:T(8,128)(2,1)S(1)}, f32[4...) custom-call(s32[2,4]{1,0:T(2,128)} %times_ref.1, s32[2]{0:T(128)} %counts_ref.1, ...), custom_call_target="tpu_custom_call" | custom-call | tf_op jit(solution)/shard_map/side/pallas_call | solution.py:491
  14.4 1.7 %collective-permute-done.2 = bf16[704,128]{1,0:T(8,128)(2,1)S(1)} collective-permute-done((bf16[704,128]{1,0:T(8,128)(2,1)S(1)}, bf16[704,128]{1,0:T(8,128)(2,1)S(1)}, u32[]{:S(2)}, u32[]{:S(2)}) %collective-permute-start.2) | collective-permute-done | bytes 180256 | tf_op jit(solution)/shard_map/ppermute | solution.py:425
  16.2 1.1 %collective-permute-start.3 = (bf16[1408,128]{1,0:T(8,128)(2,1)S(1)}, bf16[1408,128]{1,0:T(8,128)(2,1)S(1)}, u32[]{:S(2)}, u32[]{:S(2)}) collective-permute-start(bf16[1408,128]{1,0:T(8,128)(2,1)S(1)} %pad_maximum_fusion.pay_ref), channel_id=1, source_target_pairs={{0,1},{1,0},{2,3},{3,2},{4,5},{5,4},{6,7},{7,6},{8,9},{9,8},{10,11... | collective-permute-start | bytes 1081352 | tf_op jit(solution)/shard_map/ppermute | solution.py:504
  17.2 1.3 %collective-permute-done.3.pay_ref = bf16[1408,128]{1,0:T(8,128)(2,1)S(1)} collective-permute-done((bf16[1408,128]{1,0:T(8,128)(2,1)S(1)}, bf16[1408,128]{1,0:T(8,128)(2,1)S(1)}, u32[]{:S(2)}, u32[]{:S(2)}) %collective-permute-start.3) | collective-permute-done | bytes 360480 | tf_op jit(solution)/shard_map/ppermute | solution.py:504
  18.5 3.3 %solve0.1 = f32[8,64]{1,0:T(8,128)} custom-call(bf16[1408,128]{1,0:T(8,128)(2,1)S(1)} %collective-permute-done.3.pay_ref, bf16[320,64]{1,0:T(8,128)(2,1)S(1)} %get-tuple-element.28.side_ref, f32[16,128]{1,0:T(8,128)S(1)} %get-tuple-element.29.plan_ref, bf16[256,128]{1,0:T(8,128)(2,1)S(1)} %get-tuple-element.30.t2h_ref, ...), custom_call_target="tpu_custom_call" | custom-call | tf_op jit(solution)/shard_map/solve0/pallas_call | solution.py:507
  (5 shorter events, 0.1 us)
Async XLA Ops:
  0.9 5.1 %collective-permute-start = (bf16[176,128]{1,0:T(8,128)(2,1)S(1)}, bf16[176,128]{1,0:T(8,128)(2,1)S(1)}, u32[]{:S(2)}, u32[]{:S(2)}) collective-permute-start(bf16[176,128]{1,0:T(8,128)(2,1)S(1)} %fold.1), channel_id=1, source_target_pairs={{0,16},{1,9},{2,18},{3,11},{4,20},{5,13},{6,22},{7,15},{8,24},{9,1... | collective-permute-start | bytes 135176 | tf_op jit(solution)/shard_map/ppermute | solution.py:425
  6.0 4.6 %collective-permute-start.1 = (bf16[352,128]{1,0:T(8,128)(2,1)S(1)}, bf16[352,128]{1,0:T(8,128)(2,1)S(1)}, u32[]{:S(2)}, u32[]{:S(2)}) collective-permute-start(bf16[352,128]{1,0:T(8,128)(2,1)S(1)} %pad_maximum_fusion.2), channel_id=1, source_target_pairs={{0,16},{1,5},{2,18},{3,7},{4,20},{5,1},{6,22},{7,3},{8,24},{9,13},... | collective-permute-start | bytes 270344 | tf_op jit(solution)/shard_map/ppermute | solution.py:425
  10.6 5.6 %collective-permute-start.2 = (bf16[704,128]{1,0:T(8,128)(2,1)S(1)}, bf16[704,128]{1,0:T(8,128)(2,1)S(1)}, u32[]{:S(2)}, u32[]{:S(2)}) collective-permute-start(bf16[704,128]{1,0:T(8,128)(2,1)S(1)} %pad_maximum_fusion.1.pay_ref), channel_id=1, source_target_pairs={{0,16},{1,3},{2,18},{3,1},{4,20},{5,7},{6,22},{7,5},{8,24},{9,11},... | collective-permute-start | bytes 540680 | tf_op jit(solution)/shard_map/ppermute | solution.py:425
  16.2 2.4 %collective-permute-start.3 = (bf16[1408,128]{1,0:T(8,128)(2,1)S(1)}, bf16[1408,128]{1,0:T(8,128)(2,1)S(1)}, u32[]{:S(2)}, u32[]{:S(2)}) collective-permute-start(bf16[1408,128]{1,0:T(8,128)(2,1)S(1)} %pad_maximum_fusion.pay_ref), channel_id=1, source_target_pairs={{0,1},{1,0},{2,3},{3,2},{4,5},{5,4},{6,7},{7,6},{8,9},{9,8},{10,11... | collective-permute-start | bytes 1081352 | tf_op jit(solution)/shard_map/ppermute | solution.py:504

commit v4 on v3

v4 whole, which is shorter than its diff:
```python
import functools
import math

import jax
import jax.numpy as jnp
from jax import lax
from jax.experimental import pallas as pl
from jax.experimental.pallas import tpu as pltpu
from jax.sharding import PartitionSpec as P

HEAD_SIZE = 128
F32 = jnp.float32
BF16 = jnp.bfloat16
NT = (((1,), (1,)), ((), ()))
TN = (((0,), (0,)), ((), ()))


def dot(a, b, dims=(((1,), (0,)), ((), ()))):
    return lax.dot_general(a, b, dims, preferred_element_type=F32)


def split2(x):
    high = x.astype(BF16)
    return high, (x - high.astype(F32)).astype(BF16)


def split3(x):
    high = x.astype(BF16)
    mid, low = split2(x - high.astype(F32))
    return high, mid, low


def dot_fine(a, b):
    a_high, a_low = split2(a)
    b_high, b_low = split2(b)
    return dot(
        jnp.concatenate([a_high, a_high, a_low], axis=1),
        jnp.concatenate([b_high, b_low, b_high], axis=1),
        NT,
    )


def layout(channels, tokens):
    second = channels
    third = second + channels // 2
    tail = third + channels
    return second, third, tail, tail + 4 + tokens // 2 + tokens


def iotas(rows, columns):
    return (
        lax.broadcasted_iota(jnp.int32, (rows, columns), 0),
        lax.broadcasted_iota(jnp.int32, (rows, columns), 1),
    )


def fold_kernel(
    noise_hbm,
    w_in_hbm,
    wq_hbm,
    wk_hbm,
    wv_hbm,
    wo_hbm,
    wf_hbm,
    scale_hbm,
    shift_hbm,
    out_ref,
    noise,
    w_in,
    lift,
    w_a,
    w_b,
    w_c,
    wo,
    wf,
    wf2,
    scale,
    shift,
    sems,
):
    slab = lax.axis_index("slab")
    channels, width = w_in.shape
    half = channels // 2
    tokens = noise.shape[0]
    second, third, tail, rows_all = layout(channels, tokens)

    def parts(total):
        last = total[3 * channels : 3 * channels + 8]
        return (
            total[0:channels],
            total[channels : 2 * channels] + total[2 * channels : 3 * channels],
            last[0:1] + last[1:2],
        )

    @pl.when(slab == 0)
    def _():
        out_ref[...] = jnp.zeros_like(out_ref)

    @pl.when(slab != 0)
    def _():
        moves = (
            (w_in_hbm, w_in),
            (scale_hbm, scale),
            (shift_hbm, shift),
            (wf_hbm, wf),
            (wq_hbm, w_a),
            (wk_hbm, w_b),
            (wv_hbm, w_c),
            (wo_hbm, wo),
            (noise_hbm, noise),
        )
        copies = []
        for i, (src, dst) in enumerate(moves):
            copies.append(pltpu.make_async_copy(src, dst, sems.at[i]))
            copies[-1].start()
        for copy in copies[:3]:
            copy.wait()
        lift[0:channels] = w_in[...]
        high, low = split2(w_in[...].astype(F32) * scale[...].reshape(1, width))
        lift[channels : 2 * channels] = high
        lift[2 * channels : 3 * channels] = low
        shift_high, shift_low = split2(shift[...].reshape(1, width))
        row, _ = iotas(16, width)
        lift[3 * channels : 3 * channels + 16] = jnp.where(
            row == 0,
            shift_high.astype(F32),
            jnp.where(row == 1, shift_low.astype(F32), 0.0),
        ).astype(BF16)
        copies[3].wait()
        high, low = split2(wf[...])
        wf2[0:channels] = high
        wf2[channels : 2 * channels] = low
        for copy in copies[4:]:
            copy.wait()
        total = dot(lift[...], jnp.concatenate([w_a[...], w_b[...], w_c[...]], axis=1))
        both = dot(wf2[...], wo[...], NT)
        out_t = both[0:channels] + both[channels : 2 * channels]
        q0, q1, q2 = parts(total[:, 0:HEAD_SIZE] * (math.log2(math.e) / math.sqrt(HEAD_SIZE)))
        k0, k1, k2 = parts(total[:, HEAD_SIZE : 2 * HEAD_SIZE])
        v0, v1, v2 = parts(total[:, 2 * HEAD_SIZE : 3 * HEAD_SIZE])
        pad = jnp.zeros((7, HEAD_SIZE), F32)
        q_all = jnp.concatenate([q0, q1], axis=0)
        k_all = jnp.concatenate([k0, k1], axis=0)
        form = dot_fine(k_all, q_all)
        a_rows = dot_fine(jnp.concatenate([k2, pad], axis=0), q_all)
        b_rows = dot_fine(jnp.concatenate([q2, pad], axis=0), k_all)
        constant = jnp.sum(k2 * q2)
        p_rows = dot_fine(
            jnp.concatenate([v2, pad], axis=0), jnp.concatenate([out_t, out_t], axis=0)
        )
        _, lane = iotas(channels, 2 * channels)
        top, bottom = form[0:channels], form[channels : 2 * channels]
        rolled = pltpu.roll(bottom, channels, 1)
        out_ref[0:channels] = jnp.where(lane < channels, top, top + rolled).astype(BF16)
        out_ref[second:third] = jnp.where(
            lane[0:half] < channels, rolled[0:half], bottom[half:channels]
        ).astype(BF16)
        out_ref[third:tail] = dot_fine(out_t, jnp.concatenate([v0, v1], axis=0)).astype(BF16)
        n_high, n_mid, n_low = (part.astype(F32) for part in split3(noise[...]))
        lows = jnp.concatenate([n_low[0 : tokens // 2], n_low[tokens // 2 : tokens]], axis=1)
        row, lane = iotas(4, 2 * channels)
        left = lane < channels
        a_roll = pltpu.roll(a_rows, channels, 1)[0:1]
        b_roll = pltpu.roll(b_rows, channels, 1)[0:1]
        vectors = jnp.where(
            row == 0,
            jnp.where(left, 0.0, a_roll),
            jnp.where(
                row == 1,
                jnp.where(left, a_roll, constant),
                jnp.where(
                    row == 2,
                    jnp.where(left, 0.0, b_roll),
                    jnp.where(left, b_roll, p_rows[0:1]),
                ),
            ),
        )
        out_ref[tail:rows_all] = jnp.concatenate(
            [vectors, lows, jnp.concatenate([n_high, n_mid], axis=1)], axis=0
        ).astype(BF16)


def unpack(pay_ref, base, h, tables, channels, tokens):
    squares, *vectors, start = tables
    second, third, tail, rows_all = layout(channels, tokens)
    folded = pay_ref[pl.ds(base + second, third - second)].astype(F32)
    ext = pay_ref[pl.ds(base + tail, rows_all - tail)].astype(F32)
    at = pl.ds(h * channels, channels)
    squares[at] = jnp.concatenate([folded, pltpu.roll(folded, channels, 1)], axis=0).astype(BF16)
    for i, vector in enumerate(vectors):
        vector[pl.ds(h, 1)] = ext[i : i + 1]
    lows = ext[4 : 4 + tokens // 2]
    pieces = ext[4 + tokens // 2 :]
    low = jnp.concatenate([lows, pltpu.roll(lows, channels, 1)], axis=0)
    start[pl.ds(h * tokens, tokens)] = (pieces + pltpu.roll(pieces, channels, 1)) + low


def side_kernel(
    times_ref,
    counts_ref,
    w_in_ref,
    wf_ref,
    gain_ref,
    pay_ref,
    out_ref,
    plan_ref,
    *tables,
    heads,
    rows_all,
    tokens,
):
    channels, width = w_in_ref.shape
    w_in = w_in_ref[...]
    gram = dot(w_in, w_in, NT) * (1.0 / width)
    gained = w_in.astype(F32) * gain_ref[...].reshape(1, width)
    skip = dot_fine(wf_ref[...], gained)
    for h in range(heads):
        unpack(pay_ref, h * rows_all, h, tables, channels, tokens)
    g_high, g_mid, g_low = split3(gram)
    s_high, s_low = split2(skip)
    zero = jnp.zeros_like(s_high)
    out_ref[...] = jnp.concatenate(
        [
            jnp.concatenate([g_high, g_mid], axis=1),
            jnp.concatenate([s_high, s_low], axis=1),
            jnp.concatenate([g_low, zero], axis=1),
            jnp.concatenate([zero, zero], axis=1),
        ],
        axis=0,
    )

    lanes = plan_ref.shape[1]
    points = times_ref.shape[1]

    def level(slab_id, column):
        whole = jnp.zeros((1, lanes), jnp.int32) + times_ref[slab_id, column]
        return whole.astype(F32) / 1000.0

    for k in range(2):
        levels = [level(k, column) for column in range(points)]
        last = jnp.zeros((1, lanes), F32)
        for column in range(points):
            last = jnp.where(column == counts_ref[k], levels[column], last)
        steps = [
            jnp.where(j < counts_ref[k], levels[j + 1] - levels[j], 0.0)
            for j in range(points - 1)
        ]
        rows = levels + steps + [last - levels[0]]
        for i, value in enumerate(rows):
            plan_ref[pl.ds(k * 2 * points + i, 1)] = value


def solve_kernel(
    pay_ref,
    side_ref,
    plan_ref,
    *refs,
    heads,
    tokens,
    slab_id,
    ready,
    points,
):
    firsts, before_ref, out_ref, tables = refs[:6], refs[6], refs[7], refs[8:]
    squares, a_first, a_second, b_first, b_second, start = tables
    slab = lax.axis_index("slab")
    channels = side_ref.shape[1] // 2
    count = heads * tokens
    blocks = 1 + slab_id
    lanes = blocks * count
    second, third, tail, rows_all = layout(channels, tokens)
    fine_most = points - 1

    @pl.when(slab != slab_id)
    def _():
        out_ref[...] = before_ref[...]

    @pl.when(slab == slab_id)
    def _():
        for h in range(ready, heads):
            unpack(pay_ref, h * rows_all, h, tables, channels, tokens)
        if ready:
            for table, first in zip(tables[1:], firsts[1:]):
                table[0 : first.shape[0]] = first[...]

        def square(h):
            at = slice(h * channels, (h + 1) * channels)
            return firsts[0][at] if h < ready else squares[at]

        _, lane = iotas(1, lanes)
        left = lane < count
        constants = jnp.broadcast_to(a_second[:, channels : channels + 1], (heads, lanes))
        vector_maps = jnp.concatenate(
            [
                jnp.concatenate([b_first[...], a_first[...]], axis=0),
                jnp.concatenate([b_second[...], a_second[...]], axis=0),
            ],
            axis=1,
        ).astype(BF16)
        p_row = jnp.sum(b_second[...], axis=0, keepdims=True)
        p_row = jnp.broadcast_to(p_row, (8, 2 * channels))
        p_sum = jnp.broadcast_to(
            jnp.transpose(p_row)[channels : 2 * channels, 0:1], (channels, lanes)
        )
        row, column = iotas(blocks * heads, lanes)
        selectors = []
        for h in range(heads):
            if blocks == 1:
                mine = row == h
            else:
                mine = ((row == h) & (column >= count)) | ((row == heads + h) & (column < count))
            selectors.append(jnp.where(mine, 1.0, 0.0).astype(BF16))

        def level(k, column):
            row = k * 2 * points + column
            return plan_ref[row : row + 1, 0:lanes]

        def step(k, j):
            return level(k, points + j)

        def span(k):
            return level(k, 2 * points - 1)

        def by_block(row):
            if blocks == 1:
                return [row]
            return [jnp.where(left, row, 0.0), jnp.where(left, 0.0, row)]

        def key_side(rows):
            turned = jnp.transpose(rows)
            if blocks == 1:
                return turned[:, 0 : channels + heads].astype(BF16)
            first, last = turned[0:count], turned[count:lanes]
            rolled = pltpu.roll(last, channels, 1)
            terms = pltpu.roll(first, channels + heads, 1)
            _, lane = iotas(count, 2 * channels)
            one = jnp.where(lane < channels, first, rolled)
            two = jnp.where(lane < heads, rolled, terms)
            return jnp.concatenate([one, two[:, 0 : 2 * heads]], axis=1).astype(BF16)

        def velocity(u, s):
            rounded = u.astype(BF16)
            wide = rounded.astype(F32)
            s2 = s * s
            features = jnp.concatenate(
                [
                    rounded,
                    (s * wide).astype(BF16),
                    (s2 * wide).astype(BF16),
                    jnp.zeros((channels, lanes), BF16),
                ],
                axis=0,
            )
            twice = jnp.concatenate([rounded, rounded], axis=0)
            sides = dot(side_ref[0 : 2 * channels], twice) + dot(
                side_ref[2 * channels : 4 * channels], twice
            )
            norm = jnp.sum(sides[0:channels] * wide, axis=0, keepdims=True)
            r = lax.rsqrt(jnp.maximum(norm, 0.0) + 1e-06)
            maps = [vector_maps]
            for h in range(heads):
                base = h * rows_all
                maps.append(jnp.concatenate([pay_ref[base : base + channels], square(h)], axis=1))
            product = dot(jnp.concatenate(maps, axis=0), features)
            values = dot(
                jnp.concatenate(
                    [
                        pay_ref[h * rows_all + third : h * rows_all + tail]
                        for h in range(heads)
                    ],
                    axis=0,
                ),
                features[0 : 2 * channels],
            )
            offsets = r * product[heads : 2 * heads] + s2 * constants
            blank = jnp.zeros((channels - heads, lanes), F32)
            keys = key_side(jnp.concatenate([r * wide, r * product[0:heads], blank], axis=0))
            r_blocks = by_block(r)
            at_queries = 2 * heads
            rhs, pairs = [], []
            for h in range(heads):
                at = at_queries + h * channels
                raw = product[at : at + channels]
                query = [(raw * part).astype(BF16) for part in r_blocks]
                pairs.append(jnp.concatenate([*query, selectors[h]], axis=0))
            if blocks == 1:
                all_scores = [dot(keys, pair) for pair in pairs]
            else:
                joined = dot(keys, jnp.concatenate(pairs, axis=1))
                all_scores = [
                    joined[:, h * lanes : (h + 1) * lanes] for h in range(heads)
                ]
            for h in range(heads):
                scores = all_scores[h] + offsets[h : h + 1]
                raised = jnp.exp2(scores - jnp.max(scores, axis=0, keepdims=True))
                inverse = 1.0 / jnp.sum(raised, axis=0, keepdims=True)
                rhs += [(raised * part).astype(BF16) for part in by_block(inverse)]
            values = [
                (r * values[h * channels : (h + 1) * channels]).astype(BF16)
                for h in range(heads)
            ]
            mixed = dot(jnp.concatenate(values, axis=1), jnp.concatenate(rhs, axis=0))
            return (r * sides[channels : 2 * channels] + s * p_sum) + mixed

        noise = jnp.transpose(start[...])[0:channels]
        noise = jnp.concatenate([noise] * blocks, axis=1)
        moved = velocity(noise, level(0, 0))
        first_coarse = noise + span(0) * moved
        if slab_id == 0:
            u = noise + step(0, 0) * moved
            for j in range(1, fine_most):
                u = u + step(0, j) * velocity(u, level(0, j))
            ended = first_coarse + (u - first_coarse)
        else:
            u = jnp.where(left, noise + step(0, 0) * moved, first_coarse)
            coarse_old = None
            for j in range(fine_most):
                last = j == fine_most - 1
                s = jnp.where(left, level(1, 0) if last else level(0, j + 1), level(1, j))
                moved = velocity(u, s)
                if j == 0:
                    coarse_old = u + span(1) * moved
                u = u + jnp.where(left, span(1) if last else step(0, j + 1), step(1, j)) * moved
            ended = u + pltpu.roll(u - coarse_old, count, 1)
        out_ref[...] = jnp.transpose(ended)[0:tokens, 0:channels]


def exchanged(value, stride):
    groups, size, slabs = (lax.axis_size(axis) for axis in ("groups", "seq", "slab"))
    pairs = []
    for g in range(groups):
        for s in range(size):
            for c in range(slabs):
                if c == slabs - 1 or groups % 2:
                    to = (g, s ^ stride)
                else:
                    to = (g ^ 1, s)
                pairs.append(((g * size + s) * slabs + c, (to[0] * size + to[1]) * slabs + c))
    return lax.ppermute(value, ("groups", "seq", "slab"), pairs)


def local(
    noise,
    timesteps,
    fine_counts,
    w_in,
    w_query,
    w_key,
    w_value,
    w_out,
    w_final,
    mod_scale,
    mod_shift,
    skip_gain,
):
    channels, width = w_in.shape
    tokens = noise.shape[0]
    heads = lax.axis_size("seq")
    half = heads // 2
    count = tokens * heads
    points = timesteps.shape[1]
    *_, rows = layout(channels, tokens)
    wf_t = w_final.T
    vmem = pl.BlockSpec(memory_space=pltpu.VMEM)
    smem = pl.BlockSpec(memory_space=pltpu.SMEM)
    hbm = pl.BlockSpec(memory_space=pl.ANY)

    def near(*values):
        return [pltpu.with_memory_space_constraint(value, pltpu.VMEM) for value in values]

    packed = pl.pallas_call(
        fold_kernel,
        out_shape=pltpu.VMEM((rows, 2 * channels), BF16),
        in_specs=[hbm] * 9,
        out_specs=vmem,
        scratch_shapes=[
            pltpu.VMEM((tokens, channels), F32),
            pltpu.VMEM((channels, width), BF16),
            pltpu.VMEM((3 * channels + 16, width), BF16),
            pltpu.VMEM((width, HEAD_SIZE), BF16),
            pltpu.VMEM((width, HEAD_SIZE), BF16),
            pltpu.VMEM((width, HEAD_SIZE), BF16),
            pltpu.VMEM((HEAD_SIZE, width), BF16),
            pltpu.VMEM((channels, width), F32),
            pltpu.VMEM((2 * channels, width), BF16),
            pltpu.VMEM((width,), F32),
            pltpu.VMEM((width,), F32),
            pltpu.SemaphoreType.DMA((9,)),
        ],
        name="fold",
    )(noise, w_in, w_query, w_key, w_value, w_out, wf_t, mod_scale, mod_shift)
    stride = half
    own = packed
    while stride > 1:
        own = jnp.concatenate([own, exchanged(own, stride)], axis=0)
        stride //= 2

    def tables(n, kind):
        return (
            kind((n * channels, 2 * channels), BF16),
            *(kind((n, 2 * channels), F32) for _ in range(4)),
            kind((n * tokens, 2 * channels), F32),
        )

    side, plan, *firsts = pl.pallas_call(
        functools.partial(side_kernel, heads=half, rows_all=rows, tokens=tokens),
        out_shape=(
            pltpu.VMEM((4 * channels, 2 * channels), BF16),
            pltpu.VMEM((4 * points, 2 * count), F32),
            *tables(half, pltpu.VMEM),
        ),
        in_specs=[smem, smem, vmem, vmem, vmem, vmem],
        out_specs=(vmem,) * 8,
        name="side",
    )(timesteps, fine_counts, w_in, wf_t, skip_gain, *near(own))
    own = jnp.concatenate([own, exchanged(own, 1)], axis=0)
    own, side, plan, *firsts = lax.optimization_barrier((own, side, plan, *firsts))
    other = lax.ppermute(own, "slab", [(0, 1), (1, 0)])

    def solve(slab_id, pay, before, kind):
        return pl.pallas_call(
            functools.partial(
                solve_kernel,
                heads=heads,
                tokens=tokens,
                slab_id=slab_id,
                ready=half if slab_id else 0,
                points=points,
            ),
            out_shape=kind((tokens, channels), F32),
            in_specs=[vmem] * 10,
            out_specs=vmem,
            scratch_shapes=tables(heads, pltpu.VMEM),
            name=f"solve{slab_id}",
        )(*near(pay, side, plan, *firsts, before))

    ended = solve(1, own, plan[0:tokens, 0:channels], pltpu.VMEM)
    ended = solve(0, other, ended, jax.ShapeDtypeStruct)
    return ended[None]


def solution(mesh):
    placed = (
        P(("groups", "seq"), None),
        P("groups", None),
        P("groups"),
        P(),
        P(None, "seq"),
        P(None, "seq"),
        P(None, "seq"),
        P("seq", None),
        P(),
        P(),
        P(),
        P(),
    )
    return jax.shard_map(
        local,
        mesh=mesh,
        in_specs=placed,
        out_specs=P("slab", ("groups", "seq"), None),
        check_vma=False,
    )
```

time: 22.1 us -> 20.7 us (0.937)
  Pallas kernels: 5.92 us -> 4.6 us
    pallas_call x1, Pallas kernels: 0.9 us -> 0.09 us  [local(): pl.pallas_call(fold_kernel, out_shape=pltpu.VMEM((rows, 2 * channels), BF...]
    pallas_call x2, Pallas kernels: 3.3 us -> 2.77 us  [solve(): pl.pallas_call(functools.partial(solve_kernel, heads=heads, tokens=tokens...]
  transfers between devices with their start and end apart: 4 -> 4, of which waited for: 4 -> 4; matrix products, arithmetic and copies ran while one was open for 0% -> 0% of each run, Pallas kernels for 8% -> 9%
where the time goes in v4:
time: 20.7 us; the launch traced here: 20.6 us
  starting transfers between devices  8.33 us (40%)
  waiting for transfers between devices  7.55 us (36%)
  Pallas kernels  4.6 us (22%)
    ppermute x3, starting transfers between devices, exchanged(): return lax.ppermute(value, ('groups', 'seq', 'slab'), pairs)  7.2 us
    ppermute x3, waiting for transfers between devices, exchanged(): return lax.ppermute(value, ('groups', 'seq', 'slab'), pairs)  6.25 us
    pallas_call x2, Pallas kernels, solve(): pl.pallas_call(functools.partial(solve_kernel, heads=heads, tokens=tokens...  2.77 us
    pallas_call x1, Pallas kernels, local(): pl.pallas_call(functools.partial(side_kernel, heads=half, rows_all=rows,...  1.75 us
    ppermute x1, waiting for transfers between devices, local(): other = lax.ppermute(own, 'slab', [(0, 1), (1, 0)])  1.29 us
    ppermute x1, starting transfers between devices, local(): other = lax.ppermute(own, 'slab', [(0, 1), (1, 0)])  1.13 us
  transfers between devices with their start and end apart: 4, of which 4 were waited for; matrix products, arithmetic and copies ran while one was open for 0% of the time, Pallas kernels for 9%

profile of v4, /device:TPU:0, one launch (start us, length us, event | category | flops | bytes accessed | tf_op | source)
XLA Modules:
  0.0 20.6 jit_solution(3617312812809286926)
XLA Ops:
  0.0 0.1 fold.1
  0.1 3.0 %collective-permute-start = (bf16[176,128]{1,0:T(8,128)(2,1)S(1)}, bf16[176,128]{1,0:T(8,128)(2,1)S(1)}, u32[]{:S(2)}, u32[]{:S(2)}) collective-permute-start(bf16[176,128]{1,0:T(8,128)(2,1)S(1)} %fold.1), channel_id=1, source_target_pairs={{0,16},{1,9},{2,18},{3,11},{4,20},{5,13},{6,22},{7,15},{8,24},{9,1... | collective-permute-start | bytes 135176 | tf_op jit(solution)/shard_map/ppermute | solution.py:439
  3.1 2.0 %collective-permute-done = bf16[176,128]{1,0:T(8,128)(2,1)S(1)} collective-permute-done((bf16[176,128]{1,0:T(8,128)(2,1)S(1)}, bf16[176,128]{1,0:T(8,128)(2,1)S(1)}, u32[]{:S(2)}, u32[]{:S(2)}) %collective-permute-start) | collective-permute-done | bytes 45088 | tf_op jit(solution)/shard_map/ppermute | solution.py:439
  5.2 2.1 %collective-permute-start.1 = (bf16[352,128]{1,0:T(8,128)(2,1)S(1)}, bf16[352,128]{1,0:T(8,128)(2,1)S(1)}, u32[]{:S(2)}, u32[]{:S(2)}) collective-permute-start(bf16[352,128]{1,0:T(8,128)(2,1)S(1)} %pad_maximum_fusion.2), channel_id=1, source_target_pairs={{0,16},{1,5},{2,18},{3,7},{4,20},{5,1},{6,22},{7,3},{8,24},{9,13},... | collective-permute-start | bytes 270344 | tf_op jit(solution)/shard_map/ppermute | solution.py:439
  7.2 2.5 %collective-permute-done.1 = bf16[352,128]{1,0:T(8,128)(2,1)S(1)} collective-permute-done((bf16[352,128]{1,0:T(8,128)(2,1)S(1)}, bf16[352,128]{1,0:T(8,128)(2,1)S(1)}, u32[]{:S(2)}, u32[]{:S(2)}) %collective-permute-start.1) | collective-permute-done | bytes 90144 | tf_op jit(solution)/shard_map/ppermute | solution.py:439
  9.8 2.1 %collective-permute-start.2 = (bf16[704,128]{1,0:T(8,128)(2,1)S(1)}, bf16[704,128]{1,0:T(8,128)(2,1)S(1)}, u32[]{:S(2)}, u32[]{:S(2)}) collective-permute-start(bf16[704,128]{1,0:T(8,128)(2,1)S(1)} %pad_maximum_fusion.1.pay_ref), channel_id=1, source_target_pairs={{0,16},{1,3},{2,18},{3,1},{4,20},{5,7},{6,22},{7,5},{8,24},{9,11},... | collective-permute-start | bytes 540680 | tf_op jit(solution)/shard_map/ppermute | solution.py:439
  11.9 1.8 %side.1 = (bf16[256,128]{1,0:T(8,128)(2,1)S(1)}, f32[16,128]{1,0:T(8,128)S(1)}, bf16[256,128]{1,0:T(8,128)(2,1)S(1)}, f32[4,128]{1,0:T(4,128)S(1)}, f32[4,128]{1...) custom-call(s32[2,4]{1,0:T(2,128)} %times_ref.1, s32[2]{0:T(128)} %counts_ref.1, ...), custom_call_target="tpu_custom_call" | custom-call | tf_op jit(solution)/shard_map/side/pallas_call | solution.py:505
  13.6 1.7 %collective-permute-done.2 = bf16[704,128]{1,0:T(8,128)(2,1)S(1)} collective-permute-done((bf16[704,128]{1,0:T(8,128)(2,1)S(1)}, bf16[704,128]{1,0:T(8,128)(2,1)S(1)}, u32[]{:S(2)}, u32[]{:S(2)}) %collective-permute-start.2) | collective-permute-done | bytes 180256 | tf_op jit(solution)/shard_map/ppermute | solution.py:439
  15.4 1.1 %collective-permute-start.3 = (bf16[1408,128]{1,0:T(8,128)(2,1)S(1)}, bf16[1408,128]{1,0:T(8,128)(2,1)S(1)}, u32[]{:S(2)}, u32[]{:S(2)}) collective-permute-start(bf16[1408,128]{1,0:T(8,128)(2,1)S(1)} %pad_maximum_fusion.pay_ref), channel_id=1, source_target_pairs={{0,1},{1,0},{2,3},{3,2},{4,5},{5,4},{6,7},{7,6},{8,9},{9,8},{10,11... | collective-permute-start | bytes 1081352 | tf_op jit(solution)/shard_map/ppermute | solution.py:518
  16.5 1.3 %collective-permute-done.3.pay_ref = bf16[1408,128]{1,0:T(8,128)(2,1)S(1)} collective-permute-done((bf16[1408,128]{1,0:T(8,128)(2,1)S(1)}, bf16[1408,128]{1,0:T(8,128)(2,1)S(1)}, u32[]{:S(2)}, u32[]{:S(2)}) %collective-permute-start.3) | collective-permute-done | bytes 360480 | tf_op jit(solution)/shard_map/ppermute | solution.py:518
  17.8 2.8 %solve0.1 = f32[8,64]{1,0:T(8,128)} custom-call(bf16[1408,128]{1,0:T(8,128)(2,1)S(1)} %collective-permute-done.3.pay_ref, bf16[256,128]{1,0:T(8,128)(2,1)S(1)} %get-tuple-element.31.side_ref, f32[16,128]{1,0:T(8,128)S(1)} %get-tuple-element.32.plan_ref, bf16[256,128]{1,0:T(8,128)(2,1)S(1)} %get-tuple-element.33.refs_0_, ...), custom_call_target="tpu_custom_call" | custom-call | tf_op jit(solution)/shard_map/solve0/pallas_call | solution.py:521
  (5 shorter events, 0.1 us)
Async XLA Ops:
  0.1 5.1 %collective-permute-start = (bf16[176,128]{1,0:T(8,128)(2,1)S(1)}, bf16[176,128]{1,0:T(8,128)(2,1)S(1)}, u32[]{:S(2)}, u32[]{:S(2)}) collective-permute-start(bf16[176,128]{1,0:T(8,128)(2,1)S(1)} %fold.1), channel_id=1, source_target_pairs={{0,16},{1,9},{2,18},{3,11},{4,20},{5,13},{6,22},{7,15},{8,24},{9,1... | collective-permute-start | bytes 135176 | tf_op jit(solution)/shard_map/ppermute | solution.py:439
  5.2 4.6 %collective-permute-start.1 = (bf16[352,128]{1,0:T(8,128)(2,1)S(1)}, bf16[352,128]{1,0:T(8,128)(2,1)S(1)}, u32[]{:S(2)}, u32[]{:S(2)}) collective-permute-start(bf16[352,128]{1,0:T(8,128)(2,1)S(1)} %pad_maximum_fusion.2), channel_id=1, source_target_pairs={{0,16},{1,5},{2,18},{3,7},{4,20},{5,1},{6,22},{7,3},{8,24},{9,13},... | collective-permute-start | bytes 270344 | tf_op jit(solution)/shard_map/ppermute | solution.py:439
  9.8 5.6 %collective-permute-start.2 = (bf16[704,128]{1,0:T(8,128)(2,1)S(1)}, bf16[704,128]{1,0:T(8,128)(2,1)S(1)}, u32[]{:S(2)}, u32[]{:S(2)}) collective-permute-start(bf16[704,128]{1,0:T(8,128)(2,1)S(1)} %pad_maximum_fusion.1.pay_ref), channel_id=1, source_target_pairs={{0,16},{1,3},{2,18},{3,1},{4,20},{5,7},{6,22},{7,5},{8,24},{9,11},... | collective-permute-start | bytes 540680 | tf_op jit(solution)/shard_map/ppermute | solution.py:439
  15.4 2.4 %collective-permute-start.3 = (bf16[1408,128]{1,0:T(8,128)(2,1)S(1)}, bf16[1408,128]{1,0:T(8,128)(2,1)S(1)}, u32[]{:S(2)}, u32[]{:S(2)}) collective-permute-start(bf16[1408,128]{1,0:T(8,128)(2,1)S(1)} %pad_maximum_fusion.pay_ref), channel_id=1, source_target_pairs={{0,1},{1,0},{2,3},{3,2},{4,5},{5,4},{6,7},{7,6},{8,9},{9,8},{10,11... | collective-permute-start | bytes 1081352 | tf_op jit(solution)/shard_map/ppermute | solution.py:518

commit v5 on v4

--- a/solution.py
+++ b/solution.py
@@ -67,16 +67,16 @@
     out_ref,
     noise,
     w_in,
-    lift,
     w_a,
     w_b,
     w_c,
     wo,
     wf,
-    wf2,
     scale,
     shift,
     sems,
+    *,
+    pieces,
 ):
     slab = lax.axis_index("slab")
     channels, width = w_in.shape
@@ -85,12 +85,8 @@
     second, third, tail, rows_all = layout(channels, tokens)
 
     def parts(total):
-        last = total[3 * channels : 3 * channels + 8]
-        return (
-            total[0:channels],
-            total[channels : 2 * channels] + total[2 * channels : 3 * channels],
-            last[0:1] + last[1:2],
-        )
+        last = total[2 * channels : 2 * channels + 8]
+        return total[0:channels], total[channels : 2 * channels], last[0:1] + last[1:2]
 
     @pl.when(slab == 0)
     def _():
@@ -98,42 +94,50 @@
 
     @pl.when(slab != 0)
     def _():
-        moves = (
-            (w_in_hbm, w_in),
-            (scale_hbm, scale),
-            (shift_hbm, shift),
-            (wf_hbm, wf),
-            (wq_hbm, w_a),
-            (wk_hbm, w_b),
-            (wv_hbm, w_c),
-            (wo_hbm, wo),
-            (noise_hbm, noise),
-        )
-        copies = []
-        for i, (src, dst) in enumerate(moves):
-            copies.append(pltpu.make_async_copy(src, dst, sems.at[i]))
-            copies[-1].start()
-        for copy in copies[:3]:
+        used = 0
+
+        def fetch(src, dst):
+            nonlocal used
+            copy = pltpu.make_async_copy(src, dst, sems.at[used])
+            copy.start()
+            used += 1
+            return copy
+
+        waits = [fetch(w_in_hbm, w_in), fetch(scale_hbm, scale), fetch(shift_hbm, shift)]
+        tiles = width // HEAD_SIZE
+        cuts = [tiles * k // pieces // 2 * 2 * HEAD_SIZE for k in range(pieces)] + [width]
+        pulls = []
+        for low, high in zip(cuts, cuts[1:]):
+            at = pl.ds(low, high - low)
+            pulls.append(
+                [
+                    fetch(src.at[at], dst.at[at])
+                    for src, dst in ((wq_hbm, w_a), (wk_hbm, w_b), (wv_hbm, w_c))
+                ]
+            )
+        finals = [fetch(wf_hbm, wf), fetch(wo_hbm, wo), fetch(noise_hbm, noise)]
+        total = None
+        for copy in waits:
             copy.wait()
-        lift[0:channels] = w_in[...]
-        high, low = split2(w_in[...].astype(F32) * scale[...].reshape(1, width))
-        lift[channels : 2 * channels] = high
-        lift[2 * channels : 3 * channels] = low
+        factors = scale[...].reshape(1, width)
         shift_high, shift_low = split2(shift[...].reshape(1, width))
-        row, _ = iotas(16, width)
-        lift[3 * channels : 3 * channels + 16] = jnp.where(
-            row == 0,
-            shift_high.astype(F32),
-            jnp.where(row == 1, shift_low.astype(F32), 0.0),
-        ).astype(BF16)
-        copies[3].wait()
-        high, low = split2(wf[...])
-        wf2[0:channels] = high
-        wf2[channels : 2 * channels] = low
-        for copy in copies[4:]:
+        shift_high, shift_low = shift_high.astype(F32), shift_low.astype(F32)
+        for low, high, pull in zip(cuts, cuts[1:], pulls):
+            for copy in pull:
+                copy.wait()
+            at = slice(low, high)
+            plain = w_in[:, at]
+            scaled = plain.astype(F32) * factors[:, at]
+            row, _ = iotas(16, high - low)
+            vectors = jnp.where(
+                row == 0, shift_high[:, at], jnp.where(row == 1, shift_low[:, at], 0.0)
+            )
+            lift = jnp.concatenate([plain, scaled.astype(BF16), vectors.astype(BF16)], axis=0)
+            term = dot(lift, jnp.concatenate([w_a[at], w_b[at], w_c[at]], axis=1))
+            total = term if total is None else total + term
+        for copy in finals:
             copy.wait()
-        total = dot(lift[...], jnp.concatenate([w_a[...], w_b[...], w_c[...]], axis=1))
-        both = dot(wf2[...], wo[...], NT)
+        both = dot(jnp.concatenate(split2(wf[...]), axis=0), wo[...], NT)
         out_t = both[0:channels] + both[channels : 2 * channels]
         q0, q1, q2 = parts(total[:, 0:HEAD_SIZE] * (math.log2(math.e) / math.sqrt(HEAD_SIZE)))
         k0, k1, k2 = parts(total[:, HEAD_SIZE : 2 * HEAD_SIZE])
@@ -468,24 +472,23 @@
     def near(*values):
         return [pltpu.with_memory_space_constraint(value, pltpu.VMEM) for value in values]
 
+    pieces = 1
     packed = pl.pallas_call(
-        fold_kernel,
+        functools.partial(fold_kernel, pieces=pieces),
         out_shape=pltpu.VMEM((rows, 2 * channels), BF16),
         in_specs=[hbm] * 9,
         out_specs=vmem,
         scratch_shapes=[
             pltpu.VMEM((tokens, channels), F32),
             pltpu.VMEM((channels, width), BF16),
-            pltpu.VMEM((3 * channels + 16, width), BF16),
             pltpu.VMEM((width, HEAD_SIZE), BF16),
             pltpu.VMEM((width, HEAD_SIZE), BF16),
             pltpu.VMEM((width, HEAD_SIZE), BF16),
             pltpu.VMEM((HEAD_SIZE, width), BF16),
             pltpu.VMEM((channels, width), F32),
-            pltpu.VMEM((2 * channels, width), BF16),
             pltpu.VMEM((width,), F32),
             pltpu.VMEM((width,), F32),
-            pltpu.SemaphoreType.DMA((9,)),
+            pltpu.SemaphoreType.DMA((6 + 3 * pieces,)),
         ],
         name="fold",
     )(noise, w_in, w_query, w_key, w_value, w_out, wf_t, mod_scale, mod_shift)

time: 20.7 us -> 20.3 us (0.981)
  starting transfers between devices: 8.33 us -> 7.94 us
    ppermute x1, starting transfers between devices: 1.13 us -> 0.74 us  [local(): other = lax.ppermute(own, 'slab', [(0, 1), (1, 0)])]
where the time goes in v5:
time: 20.3 us; the launch traced here: 20.2 us
  starting transfers between devices  7.94 us (39%)
  waiting for transfers between devices  7.55 us (37%)
  Pallas kernels  4.6 us (23%)
    ppermute x3, starting transfers between devices, exchanged(): return lax.ppermute(value, ('groups', 'seq', 'slab'), pairs)  7.2 us
    ppermute x3, waiting for transfers between devices, exchanged(): return lax.ppermute(value, ('groups', 'seq', 'slab'), pairs)  6.25 us
    pallas_call x2, Pallas kernels, solve(): pl.pallas_call(functools.partial(solve_kernel, heads=heads, tokens=tokens...  2.76 us
    pallas_call x1, Pallas kernels, local(): pl.pallas_call(functools.partial(side_kernel, heads=half, rows_all=rows,...  1.75 us
    ppermute x1, waiting for transfers between devices, local(): other = lax.ppermute(own, 'slab', [(0, 1), (1, 0)])  1.29 us
    ppermute x1, starting transfers between devices, local(): other = lax.ppermute(own, 'slab', [(0, 1), (1, 0)])  0.74 us
  transfers between devices with their start and end apart: 4, of which 4 were waited for; matrix products, arithmetic and copies ran while one was open for 0% of the time, Pallas kernels for 9%

profile of v5, /device:TPU:0, one launch (start us, length us, event | category | flops | bytes accessed | tf_op | source)
XLA Modules:
  0.0 20.2 jit_solution(17866929783410346591)
XLA Ops:
  0.0 0.1 fold.1
  0.1 3.0 %collective-permute-start = (bf16[176,128]{1,0:T(8,128)(2,1)S(1)}, bf16[176,128]{1,0:T(8,128)(2,1)S(1)}, u32[]{:S(2)}, u32[]{:S(2)}) collective-permute-start(bf16[176,128]{1,0:T(8,128)(2,1)S(1)} %fold.1), channel_id=1, source_target_pairs={{0,16},{1,9},{2,18},{3,11},{4,20},{5,13},{6,22},{7,15},{8,24},{9,1... | collective-permute-start | bytes 135176 | tf_op jit(solution)/shard_map/ppermute | solution.py:443
  3.1 2.0 %collective-permute-done = bf16[176,128]{1,0:T(8,128)(2,1)S(1)} collective-permute-done((bf16[176,128]{1,0:T(8,128)(2,1)S(1)}, bf16[176,128]{1,0:T(8,128)(2,1)S(1)}, u32[]{:S(2)}, u32[]{:S(2)}) %collective-permute-start) | collective-permute-done | bytes 45088 | tf_op jit(solution)/shard_map/ppermute | solution.py:443
  5.2 2.1 %collective-permute-start.1 = (bf16[352,128]{1,0:T(8,128)(2,1)S(1)}, bf16[352,128]{1,0:T(8,128)(2,1)S(1)}, u32[]{:S(2)}, u32[]{:S(2)}) collective-permute-start(bf16[352,128]{1,0:T(8,128)(2,1)S(1)} %pad_maximum_fusion.2), channel_id=1, source_target_pairs={{0,16},{1,5},{2,18},{3,7},{4,20},{5,1},{6,22},{7,3},{8,24},{9,13},... | collective-permute-start | bytes 270344 | tf_op jit(solution)/shard_map/ppermute | solution.py:443
  7.2 2.5 %collective-permute-done.1 = bf16[352,128]{1,0:T(8,128)(2,1)S(1)} collective-permute-done((bf16[352,128]{1,0:T(8,128)(2,1)S(1)}, bf16[352,128]{1,0:T(8,128)(2,1)S(1)}, u32[]{:S(2)}, u32[]{:S(2)}) %collective-permute-start.1) | collective-permute-done | bytes 90144 | tf_op jit(solution)/shard_map/ppermute | solution.py:443
  9.8 2.1 %collective-permute-start.2 = (bf16[704,128]{1,0:T(8,128)(2,1)S(1)}, bf16[704,128]{1,0:T(8,128)(2,1)S(1)}, u32[]{:S(2)}, u32[]{:S(2)}) collective-permute-start(bf16[704,128]{1,0:T(8,128)(2,1)S(1)} %pad_maximum_fusion.1.pay_ref), channel_id=1, source_target_pairs={{0,16},{1,3},{2,18},{3,1},{4,20},{5,7},{6,22},{7,5},{8,24},{9,11},... | collective-permute-start | bytes 540680 | tf_op jit(solution)/shard_map/ppermute | solution.py:443
  11.9 1.8 %side.1 = (bf16[256,128]{1,0:T(8,128)(2,1)S(1)}, f32[16,128]{1,0:T(8,128)S(1)}, bf16[256,128]{1,0:T(8,128)(2,1)S(1)}, f32[4,128]{1,0:T(4,128)S(1)}, f32[4,128]{1...) custom-call(s32[2,4]{1,0:T(2,128)} %times_ref.1, s32[2]{0:T(128)} %counts_ref.1, ...), custom_call_target="tpu_custom_call" | custom-call | tf_op jit(solution)/shard_map/side/pallas_call | solution.py:508
  13.6 1.7 %collective-permute-done.2 = bf16[704,128]{1,0:T(8,128)(2,1)S(1)} collective-permute-done((bf16[704,128]{1,0:T(8,128)(2,1)S(1)}, bf16[704,128]{1,0:T(8,128)(2,1)S(1)}, u32[]{:S(2)}, u32[]{:S(2)}) %collective-permute-start.2) | collective-permute-done | bytes 180256 | tf_op jit(solution)/shard_map/ppermute | solution.py:443
  15.4 0.7 %collective-permute-start.3 = (bf16[1408,128]{1,0:T(8,128)(2,1)S(1)}, bf16[1408,128]{1,0:T(8,128)(2,1)S(1)}, u32[]{:S(2)}, u32[]{:S(2)}) collective-permute-start(bf16[1408,128]{1,0:T(8,128)(2,1)S(1)} %pad_maximum_fusion.pay_ref), channel_id=1, source_target_pairs={{0,1},{1,0},{2,3},{3,2},{4,5},{5,4},{6,7},{7,6},{8,9},{9,8},{10,11... | collective-permute-start | bytes 1081352 | tf_op jit(solution)/shard_map/ppermute | solution.py:521
  16.1 1.3 %collective-permute-done.3.pay_ref = bf16[1408,128]{1,0:T(8,128)(2,1)S(1)} collective-permute-done((bf16[1408,128]{1,0:T(8,128)(2,1)S(1)}, bf16[1408,128]{1,0:T(8,128)(2,1)S(1)}, u32[]{:S(2)}, u32[]{:S(2)}) %collective-permute-start.3) | collective-permute-done | bytes 360480 | tf_op jit(solution)/shard_map/ppermute | solution.py:521
  17.4 2.8 %solve0.1 = f32[8,64]{1,0:T(8,128)} custom-call(bf16[1408,128]{1,0:T(8,128)(2,1)S(1)} %collective-permute-done.3.pay_ref, bf16[256,128]{1,0:T(8,128)(2,1)S(1)} %get-tuple-element.31.side_ref, f32[16,128]{1,0:T(8,128)S(1)} %get-tuple-element.32.plan_ref, bf16[256,128]{1,0:T(8,128)(2,1)S(1)} %get-tuple-element.33.refs_0_, ...), custom_call_target="tpu_custom_call" | custom-call | tf_op jit(solution)/shard_map/solve0/pallas_call | solution.py:524
  (5 shorter events, 0.1 us)
Async XLA Ops:
  0.1 5.1 %collective-permute-start = (bf16[176,128]{1,0:T(8,128)(2,1)S(1)}, bf16[176,128]{1,0:T(8,128)(2,1)S(1)}, u32[]{:S(2)}, u32[]{:S(2)}) collective-permute-start(bf16[176,128]{1,0:T(8,128)(2,1)S(1)} %fold.1), channel_id=1, source_target_pairs={{0,16},{1,9},{2,18},{3,11},{4,20},{5,13},{6,22},{7,15},{8,24},{9,1... | collective-permute-start | bytes 135176 | tf_op jit(solution)/shard_map/ppermute | solution.py:443
  5.2 4.6 %collective-permute-start.1 = (bf16[352,128]{1,0:T(8,128)(2,1)S(1)}, bf16[352,128]{1,0:T(8,128)(2,1)S(1)}, u32[]{:S(2)}, u32[]{:S(2)}) collective-permute-start(bf16[352,128]{1,0:T(8,128)(2,1)S(1)} %pad_maximum_fusion.2), channel_id=1, source_target_pairs={{0,16},{1,5},{2,18},{3,7},{4,20},{5,1},{6,22},{7,3},{8,24},{9,13},... | collective-permute-start | bytes 270344 | tf_op jit(solution)/shard_map/ppermute | solution.py:443
  9.8 5.6 %collective-permute-start.2 = (bf16[704,128]{1,0:T(8,128)(2,1)S(1)}, bf16[704,128]{1,0:T(8,128)(2,1)S(1)}, u32[]{:S(2)}, u32[]{:S(2)}) collective-permute-start(bf16[704,128]{1,0:T(8,128)(2,1)S(1)} %pad_maximum_fusion.1.pay_ref), channel_id=1, source_target_pairs={{0,16},{1,3},{2,18},{3,1},{4,20},{5,7},{6,22},{7,5},{8,24},{9,11},... | collective-permute-start | bytes 540680 | tf_op jit(solution)/shard_map/ppermute | solution.py:443
  15.4 2.0 %collective-permute-start.3 = (bf16[1408,128]{1,0:T(8,128)(2,1)S(1)}, bf16[1408,128]{1,0:T(8,128)(2,1)S(1)}, u32[]{:S(2)}, u32[]{:S(2)}) collective-permute-start(bf16[1408,128]{1,0:T(8,128)(2,1)S(1)} %pad_maximum_fusion.pay_ref), channel_id=1, source_target_pairs={{0,1},{1,0},{2,3},{3,2},{4,5},{5,4},{6,7},{7,6},{8,9},{9,8},{10,11... | collective-permute-start | bytes 1081352 | tf_op jit(solution)/shard_map/ppermute | solution.py:521
